TPU v7x, 512 devices: a whole 4x8x8 slice. The times are simulated.
512 devices in a mesh: group: 16 (over z, core), dp: 32 (over x, y).
Axes of the slice: x: 4, y: 8, z: 8, core: 2. Of those that a mesh axis runs over, the one named last changes fastest.
Arguments:
- queries: bfloat16 [1024, 128, 512], P(('group', 'dp')), may hold values from -256 to 256
- passages: bfloat16 [3072, 128, 512], P(('group', 'dp')), may hold values from -6 to 6
- candidates: int32 [1024, 16], replicated, may hold values from 0 to 3071, as said below
- positives: int32 [1024, 128], P(('group', 'dp')), may hold values from 0 to 2047
- row_weight: float32 [1024, 128], P(('group', 'dp')), may hold values from 0.25 to 4
- owner_map: int32 [3072], replicated, may hold values from 0 to 3071, as said below
Outputs:
- grad_query: bfloat16 [1024, 128, 512], P(('group', 'dp'))
- grad_passage: bfloat16 [3072, 128, 512], P(('group', 'dp'))
Inputs may be any that keep to these rules, and one draw needn't show every extreme that they name: `owner_map`: A permutation: entry i is the row block of passages that holds block id i. `candidates`: each row lists 16 different block ids: 12 held by devices of the query block's own group, the others held by devices of other groups with the same dp index. Over all query blocks of one device, at most 1 distinct listed blocks lie on any one device of its group and at most 1 on the devices of any one other group; for every device both bounds are reached.
All inputs are finite; a program needn't handle non-finite values.
Results may differ from a plain program's by a relative error of at most 0.0057.
Values may be sent and summed in bfloat16 or wider, within the bound.
A program may use at most 128 MiB of HBM per device.

v0:
```python
import math

import jax
import jax.numpy as jnp
from jax import lax
from jax.sharding import PartitionSpec as P

NLOCAL = 12


def route_plan(
    listed_rows, home_group, owner_map, owned_blocks, dp_size, group_size, local_cap, remote_cap
):
    listed_ids = listed_rows.reshape(-1)
    count = listed_ids.shape[0]
    positions = jnp.take(owner_map, listed_ids)
    owner = positions // owned_blocks
    block_slot = positions % owned_blocks
    owner_group = owner // dp_size
    owner_column = owner % dp_size
    is_local = owner_group == home_group
    peer = jnp.where(is_local, owner_column, owner_group)
    listing = jnp.arange(count, dtype=jnp.int32)
    same_block = listed_ids[:, None] == listed_ids[None, :]
    earlier = same_block & (listing[None, :] < listing[:, None])
    unique = jnp.logical_not(jnp.any(earlier, axis=1))
    first_seen = jnp.min(jnp.where(same_block, listing[None, :], count), axis=1)
    ahead = (
        (peer[None, :] == peer[:, None])
        & (is_local[None, :] == is_local[:, None])
        & unique[None, :]
        & (listing[None, :] < first_seen[:, None])
    )
    slot_rank = jnp.sum(ahead.astype(jnp.int32), axis=1)
    local_index = jnp.clip(owner_column * local_cap + slot_rank, 0, dp_size * local_cap - 1)
    remote_index = jnp.clip(owner_group * remote_cap + slot_rank, 0, group_size * remote_cap - 1)
    payload = jnp.where(unique, block_slot + 1, 0)
    local_hit = (
        is_local[:, None, None]
        & (owner_column[:, None, None] == jnp.arange(dp_size, dtype=jnp.int32)[None, :, None])
        & (slot_rank[:, None, None] == jnp.arange(local_cap, dtype=jnp.int32)[None, None, :])
    )
    local_table = jnp.sum(jnp.where(local_hit, payload[:, None, None], 0), axis=0) - 1
    remote_hit = (
        jnp.logical_not(is_local)[:, None, None]
        & (owner_group[:, None, None] == jnp.arange(group_size, dtype=jnp.int32)[None, :, None])
        & (slot_rank[:, None, None] == jnp.arange(remote_cap, dtype=jnp.int32)[None, None, :])
    )
    remote_table = jnp.sum(jnp.where(remote_hit, payload[:, None, None], 0), axis=0) - 1
    return (is_local, local_index, remote_index, local_table, remote_table)


def serve_blocks(table, passages):
    valid = table >= 0
    blocks = jnp.take(passages, jnp.maximum(table, 0), axis=0)
    return jnp.where(valid[..., None, None], blocks, jnp.zeros_like(blocks))


def shards(queries, passages, candidates, positives, row_weight, owner_map):
    dp_size = lax.axis_size("dp")
    group_size = lax.axis_size("group")
    my_group = lax.axis_index("group")
    my_column = lax.axis_index("dp")
    query_blocks, block_rows, width = queries.shape
    owned_blocks = passages.shape[0]
    cand_count = candidates.shape[1]
    local_cap = (NLOCAL + dp_size - 1) // dp_size
    remote_cap = (cand_count - NLOCAL + group_size - 2) // (group_size - 1)
    local_slots_all = dp_size * local_cap
    total_slots = local_slots_all + group_size * remote_cap
    all_lists = candidates.reshape(group_size, dp_size, query_blocks, cand_count)

    def plan_for(listed_rows, home_group):
        return route_plan(
            listed_rows,
            home_group,
            owner_map,
            owned_blocks,
            dp_size,
            group_size,
            local_cap,
            remote_cap,
        )

    my_lists = all_lists[my_group, my_column]
    is_local, local_index, remote_index, own_local, own_remote = plan_for(my_lists, my_group)
    peers_local = jax.vmap(plan_for, in_axes=(0, None))(all_lists[my_group], my_group)[3]
    peers_remote = jax.vmap(plan_for)(
        all_lists[:, my_column], jnp.arange(group_size, dtype=jnp.int32)
    )[4]
    asked_local = jnp.take(peers_local, my_column, axis=1)
    asked_remote = jnp.take(peers_remote, my_group, axis=1)
    local_buffer = lax.all_to_all(
        serve_blocks(asked_local, passages), "dp", split_axis=0, concat_axis=0, tiled=True
    )
    remote_buffer = lax.all_to_all(
        serve_blocks(asked_remote, passages), "group", split_axis=0, concat_axis=0, tiled=True
    )
    local_flat = local_buffer.reshape(local_slots_all, block_rows, width)
    remote_flat = remote_buffer.reshape(group_size * remote_cap, block_rows, width)
    score_scale = 3.0 / math.sqrt(width)
    slot_index = jnp.where(is_local, local_index, local_slots_all + remote_index)
    slot_grid = slot_index.reshape(query_blocks, cand_count)
    pool = jnp.concatenate([local_flat, remote_flat], axis=0)
    candidate = jnp.take(pool, slot_index, axis=0).reshape(
        query_blocks, cand_count, block_rows, width
    )
    scores = (
        jnp.einsum("brd,bkjd->brkj", queries, candidate, preferred_element_type=jnp.float32)
        * score_scale
    )
    flat_scores = scores.reshape(query_blocks, block_rows, cand_count * block_rows)
    probability = jax.nn.softmax(flat_scores, axis=-1)
    target = (
        jnp.arange(cand_count * block_rows, dtype=jnp.int32)[None, None, :] == positives[:, :, None]
    ).astype(jnp.float32)
    dscore = ((probability - target) * (row_weight[:, :, None] * score_scale)).astype(jnp.bfloat16)
    dscore = dscore.reshape(query_blocks, block_rows, cand_count, block_rows)
    grad_query = jnp.einsum(
        "brkj,bkjd->brd", dscore, candidate, preferred_element_type=jnp.float32
    ).astype(jnp.bfloat16)

    def add_block(index, totals):
        block_terms = jnp.einsum(
            "rkj,rd->kjd", dscore[index], queries[index], preferred_element_type=jnp.float32
        )
        return totals.at[slot_grid[index]].add(block_terms)

    slot_terms = lax.fori_loop(
        0, query_blocks, add_block, jnp.zeros((total_slots, block_rows, width), jnp.float32)
    )
    slot_terms = slot_terms.astype(jnp.bfloat16)
    local_out = slot_terms[:local_slots_all].reshape(dp_size, local_cap, block_rows, width)
    remote_out = slot_terms[local_slots_all:].reshape(group_size, remote_cap, block_rows, width)
    local_back = lax.all_to_all(local_out, "dp", split_axis=0, concat_axis=0, tiled=True)
    remote_back = lax.all_to_all(remote_out, "group", split_axis=0, concat_axis=0, tiled=True)
    owned = jnp.arange(owned_blocks, dtype=jnp.int32)
    local_owner = (asked_local[..., None] == owned).astype(jnp.bfloat16)
    remote_owner = (asked_remote[..., None] == owned).astype(jnp.bfloat16)
    grad_sum = jnp.einsum(
        "qcp,qcxd->pxd", local_owner, local_back, preferred_element_type=jnp.float32
    )
    grad_sum = grad_sum + jnp.einsum(
        "qcp,qcxd->pxd", remote_owner, remote_back, preferred_element_type=jnp.float32
    )
    return (grad_query, grad_sum.astype(jnp.bfloat16))


def solution(mesh):
    return jax.shard_map(
        shards,
        mesh=mesh,
        in_specs=(
            P(("group", "dp"), None, None),
            P(("group", "dp"), None, None),
            P(),
            P(("group", "dp"), None),
            P(("group", "dp"), None),
            P(),
        ),
        out_specs=(P(("group", "dp"), None, None), P(("group", "dp"), None, None)),
        check_vma=False,
    )
```

profile of v0, /device:TPU:6, one launch (start us, length us, event | category | flops | bytes accessed | tf_op | source)
XLA Modules:
  0.0 393.8 jit_solution(5141496502204511688)
XLA Ops:
  0.7 1.1 copy.108
  3.0 3.1 gather_fusion.3
  8.2 1.6 fusion.17
  9.8 10.4 %all-to-all-start.1 = ((bf16[16,1,128,512]{3,2,1,0:T(8,128)(2,1)}), bf16[16,1,128,512]{3,2,1,0:T(8,128)(2,1)S(1)}, u32[]{:S(2)}, u32[]{:S(2)}) async-start(bf16[16,1,128,512]{3,2,1,0:T(8,128)(2,1)} %fusion.17), calls=%async_computation.1 | async-start | bytes 4194304 | tf_op jit(solution)/shard_map/all_to_all | solution.py:96
  21.4 0.8 fusion.30
  22.4 6.2 %gather_fusion.1 = s32[1024]{0:T(1024)S(1)} fusion(s32[3072]{0:T(1024)S(1)} %copy-done.2, s32[1024]{0:T(1024)S(1)} %broadcast_clamp_fusion), kind=kCustom, calls=%fused_computation.1 | custom fusion | bytes 12288 | tf_op jit(solution)/shard_map/vmap(jit(_take))/gather | solution.py:16
  29.5 1.2 convert_reduce_fusion
  31.6 2.7 gather_fusion.2
  34.4 4.6 %fusion.10 = bf16[32,1,128,512]{3,2,1,0:T(8,128)(2,1)} fusion(bf16[32,128,512]{2,1,0:T(8,128)(2,1)} %gather_fusion.2, pred[32]{0:T(512)(128)(4,1)S(1)} %get-tuple-element.165, pred[32]{0:T(512)(128)(4,1)S(1)} %get-tuple-element.166), kind=kLoop, calls=%fused_computation.22 | loop fusion | flops 4194304 | bytes 8388672 | tf_op jit(solution)/shard_map/jit(_where)/select_n | solution.py:56
  39.0 30.4 %all-to-all-done.1 = bf16[16,1,128,512]{3,2,1,0:T(8,128)(2,1)S(1)} async-done(((bf16[16,1,128,512]{3,2,1,0:T(8,128)(2,1)}), bf16[16,1,128,512]{3,2,1,0:T(8,128)(2,1)S(1)}, u32[]{:S(2)}, u32[]{:S(2)}) %all-to-all-start.1) | async-done | bytes 2097184 | tf_op jit(solution)/shard_map/all_to_all | solution.py:96
  69.5 10.3 %all-to-all-start = ((bf16[32,1,128,512]{3,2,1,0:T(8,128)(2,1)}), bf16[32,1,128,512]{3,2,1,0:T(8,128)(2,1)}, u32[]{:S(2)}, u32[]{:S(2)}) async-start(bf16[32,1,128,512]{3,2,1,0:T(8,128)(2,1)} %fusion.10), calls=%async_computation | async-start | bytes 8388608 | tf_op jit(solution)/shard_map/all_to_all | solution.py:93
  81.0 93.9 %all-to-all-done = bf16[32,1,128,512]{3,2,1,0:T(8,128)(2,1)} async-done(((bf16[32,1,128,512]{3,2,1,0:T(8,128)(2,1)}), bf16[32,1,128,512]{3,2,1,0:T(8,128)(2,1)}, u32[]{:S(2)}, u32[]{:S(2)}) %all-to-all-start) | async-done | bytes 4194336 | tf_op jit(solution)/shard_map/all_to_all | solution.py:93
  174.8 5.4 %pad_maximum_fusion = bf16[48,128,512]{2,1,0:T(8,128)(2,1)} fusion(bf16[16,128,512]{2,1,0:T(8,128)(2,1)S(1)} %bitcast.95, bf16[32,128,512]{2,1,0:T(8,128)(2,1)} %bitcast.10), kind=kLoop, calls=%fused_computation.17 | loop fusion | flops 3145728 | bytes 12582912 | tf_op jit(solution)/shard_map/concatenate | solution.py:104
  180.2 5.7 %gather_fusion.5 = bf16[32,128,512]{2,1,0:T(8,128)(2,1)} fusion(bf16[48,128,512]{2,1,0:T(8,128)(2,1)} %pad_maximum_fusion, s32[1024]{0:T(1024)S(1)} %pad_clamp_fusion), kind=kCustom, calls=%fused_computation.5 | custom fusion | bytes 8388736 | tf_op jit(solution)/shard_map/jit(_take)/gather | solution.py:105
  185.9 3.5 bitcast_reduce_fusion
  190.6 6.2 %broadcast_in_dim.242 = f32[48,128,512]{2,1,0:T(8,128)} broadcast(f32[]{:T(128)} %constant.275.clone.1), dimensions={} | broadcast | bytes 12582916 | tf_op jit(solution)/shard_map/broadcast_in_dim | solution.py:130
  196.7 24.8 %while.15 = (s32[]{:T(128)}, f32[48,128,512]{2,1,0:T(8,128)}, s32[2,16]{1,0:T(2,128)S(1)}, bf16[2,128,16,128]{1,3,2,0:T(8,128)(2,1)S(1)}, bf16[2,128,512]{2,1,0:T(8,128)(2,1)S(1)}, /*index=5*/s32[]{:T(128)}) while((s32[]{:T(128)}, f32[48,128,512]{2,1,0:T(8,128)}, s32[2,16]{1,0:T(2,128)S(1)}, bf16[2,128,16,128]{1,3,2,0:T(8,128)(2,1)S(1)}, ...), condition=%wide.region_15.16_spmd, body=%wide.region_13.15_spmd.sunk | while | flops 269484096 | bytes 17433872 | solution.py:129
  196.8 2.6 fusion.82
  199.4 9.8 %scatter_fusion = f32[48,128,512]{2,1,0:T(8,128)} fusion(f32[48,128,512]{2,1,0:T(8,128)} %get-tuple-element.205, s32[16]{0:T(128)S(1)} %fusion.81, f32[16,128,512]{2,1,0:T(8,128)} %fusion.82), kind=kCustom, calls=%fused_computation.6.clone.1 | custom fusion | flops 1048576 | bytes 12582976 | tf_op jit(solution)/shard_map/while/body/eval_jaxpr/scatter-add | solution.py:127
  209.2 2.6 fusion.82
  211.9 9.7 %scatter_fusion = f32[48,128,512]{2,1,0:T(8,128)} fusion(f32[48,128,512]{2,1,0:T(8,128)} %get-tuple-element.205, s32[16]{0:T(128)S(1)} %fusion.81, f32[16,128,512]{2,1,0:T(8,128)} %fusion.82), kind=kCustom, calls=%fused_computation.6.clone.1 | custom fusion | flops 1048576 | bytes 12582976 | tf_op jit(solution)/shard_map/while/body/eval_jaxpr/scatter-add | solution.py:127
  221.6 8.2 %convert_element_type.34 = bf16[48,128,512]{2,1,0:T(8,128)(2,1)} convert(f32[48,128,512]{2,1,0:T(8,128)} %get-tuple-element.96) | non-fusion elementwise | flops 3145728 | bytes 18874368 | tf_op jit(solution)/shard_map/convert_element_type | solution.py:132
  229.7 4.6 %slice_bitcast_fusion = bf16[32,1,128,512]{3,2,1,0:T(8,128)(2,1)} fusion(bf16[48,128,512]{2,1,0:T(8,128)(2,1)} %convert_element_type.34), kind=kLoop, calls=%fused_computation.18 | loop fusion | bytes 8388608 | tf_op jit(solution)/shard_map/reshape | solution.py:133
  234.3 7.1 %all-to-all-start.2 = ((bf16[32,1,128,512]{3,2,1,0:T(8,128)(2,1)}), bf16[32,1,128,512]{3,2,1,0:T(8,128)(2,1)}, u32[]{:S(2)}, u32[]{:S(2)}) async-start(bf16[32,1,128,512]{3,2,1,0:T(8,128)(2,1)} %slice_bitcast_fusion), calls=%async_computation.2 | async-start | bytes 8388608 | tf_op jit(solution)/shard_map/all_to_all | solution.py:135
  241.4 3.2 slice_bitcast_fusion.1
  244.6 91.1 %all-to-all-done.2 = bf16[32,1,128,512]{3,2,1,0:T(8,128)(2,1)} async-done(((bf16[32,1,128,512]{3,2,1,0:T(8,128)(2,1)}), bf16[32,1,128,512]{3,2,1,0:T(8,128)(2,1)}, u32[]{:S(2)}, u32[]{:S(2)}) %all-to-all-start.2) | async-done | bytes 4194336 | tf_op jit(solution)/shard_map/all_to_all | solution.py:135
  335.7 4.8 %all-to-all-start.3 = ((bf16[16,1,128,512]{3,2,1,0:T(8,128)(2,1)}), bf16[16,1,128,512]{3,2,1,0:T(8,128)(2,1)}, u32[]{:S(2)}, u32[]{:S(2)}) async-start(bf16[16,1,128,512]{3,2,1,0:T(8,128)(2,1)} %slice_bitcast_fusion.1), calls=%async_computation.3 | async-start | bytes 4194304 | tf_op jit(solution)/shard_map/all_to_all | solution.py:136
  340.5 3.7 fusion.25
  344.2 4.6 %fusion.8 = f32[6,128,512]{2,0,1:T(8,128)S(1)} fusion(bf16[32,1,128,512]{3,2,1,0:T(8,128)(2,1)} %all-to-all-done.2, s32[32]{0:T(128)S(1)} %get-tuple-element.131), kind=kOutput, calls=%fused_computation.19 | convolution fusion | flops 25166016 | bytes 5767296 | tf_op jit(solution)/shard_map/qcp,qcxd->pxd/dot_general | solution.py:140
  348.9 40.9 %all-to-all-done.3 = bf16[16,1,128,512]{3,2,1,0:T(8,128)(2,1)} async-done(((bf16[16,1,128,512]{3,2,1,0:T(8,128)(2,1)}), bf16[16,1,128,512]{3,2,1,0:T(8,128)(2,1)}, u32[]{:S(2)}, u32[]{:S(2)}) %all-to-all-start.3) | async-done | bytes 2097184 | tf_op jit(solution)/shard_map/all_to_all | solution.py:136
  389.8 2.9 add_convert_fusion
  392.7 1.1 copy.127
  (74 shorter events, 8.6 us)
Async XLA Ops:
  0.6 6.9 %copy-start = (bf16[6,128,512]{2,1,0:T(8,128)(2,1)S(1)}, bf16[6,128,512]{2,1,0:T(8,128)(2,1)}, u32[]{:S(2)}) copy-start(bf16[6,128,512]{2,1,0:T(8,128)(2,1)} %param.9) | copy-start | bytes 2359300
  0.6 2.4 copy-start.2
  9.8 59.7 %all-to-all-start.1 = ((bf16[16,1,128,512]{3,2,1,0:T(8,128)(2,1)}), bf16[16,1,128,512]{3,2,1,0:T(8,128)(2,1)S(1)}, u32[]{:S(2)}, u32[]{:S(2)}) async-start(bf16[16,1,128,512]{3,2,1,0:T(8,128)(2,1)} %fusion.17), calls=%async_computation.1 | async-start | bytes 4194304 | tf_op jit(solution)/shard_map/all_to_all | solution.py:96
  39.0 41.9 %copy-start.5 = (f32[2,128]{1,0:T(2,128)S(1)}, f32[2,128]{1,0:T(2,128)}, u32[]{:S(2)}) copy-start(f32[2,128]{1,0:T(2,128)} %param.12) | copy-start | bytes 3076
  69.5 105.3 %all-to-all-start = ((bf16[32,1,128,512]{3,2,1,0:T(8,128)(2,1)}), bf16[32,1,128,512]{3,2,1,0:T(8,128)(2,1)}, u32[]{:S(2)}, u32[]{:S(2)}) async-start(bf16[32,1,128,512]{3,2,1,0:T(8,128)(2,1)} %fusion.10), calls=%async_computation | async-start | bytes 8388608 | tf_op jit(solution)/shard_map/all_to_all | solution.py:93
  180.2 5.7 %copy-start.3 = (bf16[2,128,512]{2,1,0:T(8,128)(2,1)S(1)}, bf16[2,128,512]{2,1,0:T(8,128)(2,1)}, u32[]{:S(2)}) copy-start(bf16[2,128,512]{2,1,0:T(8,128)(2,1)} %param.8) | copy-start | bytes 786436
  185.9 3.9 copy-start.4
  234.3 101.4 %all-to-all-start.2 = ((bf16[32,1,128,512]{3,2,1,0:T(8,128)(2,1)}), bf16[32,1,128,512]{3,2,1,0:T(8,128)(2,1)}, u32[]{:S(2)}, u32[]{:S(2)}) async-start(bf16[32,1,128,512]{3,2,1,0:T(8,128)(2,1)} %slice_bitcast_fusion), calls=%async_computation.2 | async-start | bytes 8388608 | tf_op jit(solution)/shard_map/all_to_all | solution.py:135
  335.7 54.1 %all-to-all-start.3 = ((bf16[16,1,128,512]{3,2,1,0:T(8,128)(2,1)}), bf16[16,1,128,512]{3,2,1,0:T(8,128)(2,1)}, u32[]{:S(2)}, u32[]{:S(2)}) async-start(bf16[16,1,128,512]{3,2,1,0:T(8,128)(2,1)} %slice_bitcast_fusion.1), calls=%async_computation.3 | async-start | bytes 4194304 | tf_op jit(solution)/shard_map/all_to_all | solution.py:136
  344.2 49.6 %copy-start.1 = (bf16[6,128,512]{2,1,0:T(8,128)(2,1)S(1)}, bf16[6,128,512]{2,1,0:T(8,128)(2,1)}, u32[]{:S(2)}) copy-start(bf16[6,128,512]{2,1,0:T(8,128)(2,1)} %param.9) | copy-start | bytes 2359300
where the time goes:
time: 398 us; the launch traced here: 394 us
  waiting for transfers between devices  256 us (64%)
  other arithmetic  47.3 us (12%)
  local copies, waits for them, and re-layouts  36.5 us (9%)
  starting transfers between devices  32.6 us (8%)
  matrix products  20.1 us (5%)
    all_to_all x1, waiting for transfers between devices, shards(): lax.all_to_all(serve_blocks(asked_local, passages), 'dp', split_axis=0, c...  93.9 us
    all_to_all x1, waiting for transfers between devices, shards(): lax.all_to_all(local_out, 'dp', split_axis=0, concat_axis=0, tiled=True)  91.1 us
    all_to_all x1, waiting for transfers between devices, shards(): lax.all_to_all(remote_out, 'group', split_axis=0, concat_axis=0, tiled=True)  40.9 us
    all_to_all x1, waiting for transfers between devices, shards(): lax.all_to_all(serve_blocks(asked_remote, passages), 'group', split_axis=...  30.4 us
    scatter-add x2, other arithmetic, add_block(): return totals.at[slot_grid[index]].add(block_terms)  19.5 us
    all_to_all x1, starting transfers between devices, shards(): lax.all_to_all(serve_blocks(asked_remote, passages), 'group', split_axis=...  10.4 us
    gather x7, local copies, waits for them, and re-layouts, route_plan(): positions = jnp.take(owner_map, listed_ids)  10.3 us
    all_to_all x1, starting transfers between devices, shards(): lax.all_to_all(serve_blocks(asked_local, passages), 'dp', split_axis=0, c...  10.3 us
  transfers between devices with their start and end apart: 4, of which 4 were waited for; matrix products, arithmetic and copies ran while one was open for 8% of the time, Pallas kernels for 0%

commit v1 on v0

v1 whole, which is shorter than its diff:
```python
import functools
import math

import jax
import jax.numpy as jnp
from jax import lax
from jax.experimental import pallas as pl
from jax.experimental.pallas import tpu as pltpu
from jax.sharding import PartitionSpec as P

MESH = pl.DeviceIdType.MESH
NEG = -1e30
CORES = 2
SIZES = (4, 8)


def scratch_plan(nx, ny, nz, qb, owned, rows, width):
    lanes = qb * rows
    dma = pltpu.SemaphoreType.DMA
    bf, f32 = jnp.bfloat16, jnp.float32
    hy, hz, hx = max(ny // 2, 1), max(nz // 2, 1), max(nx // 2, 1)
    plan = {
        "qy": pltpu.VMEM((ny, lanes, width), bf),
        "qz": pltpu.VMEM((nz, lanes, width), bf),
        "pc": pltpu.VMEM((owned, rows, width), bf),
        "tab": pltpu.SMEM(((nx * ny + CORES * nz) * 3,), jnp.int32),
        "auxy": pltpu.VMEM((ny, 8, lanes), f32),
        "auxz": pltpu.VMEM((nz, 8, lanes), f32),
        "e": pltpu.VMEM((nx * ny + CORES * nz, rows, lanes), f32),
        "d": pltpu.VMEM((nx * ny + CORES * nz, rows, lanes), bf),
        "my": pltpu.VMEM((nx, ny, lanes), f32),
        "sy": pltpu.VMEM((nx, ny, lanes), f32),
        "mz": pltpu.VMEM((CORES, nz, lanes), f32),
        "sz": pltpu.VMEM((CORES, nz, lanes), f32),
        "zst": pltpu.VMEM((nz, lanes), f32),
        "zsr": pltpu.VMEM((nz, nz, lanes), f32),
        "yst": pltpu.VMEM((ny, lanes), f32),
        "ysr": pltpu.VMEM((ny, ny, lanes), f32),
        "ya": pltpu.VMEM((ny, lanes), f32),
        "fin": pltpu.VMEM((8, lanes), f32),
        "zfr": pltpu.VMEM((nz, 8, lanes), f32),
        "t": pltpu.VMEM((max(ny, nz), rows, width), f32),
        "gqy": pltpu.VMEM((ny, lanes, width), f32),
        "gqz": pltpu.VMEM((nz, lanes, width), f32),
        "gp": pltpu.VMEM((nx + CORES, owned, rows, width), f32),
        "yo": pltpu.VMEM((2, hy, qb, rows, width), bf),
        "yi": pltpu.VMEM((2, hy, qb, rows, width), bf),
        "zo": pltpu.VMEM((2, hz, qb, rows, width), bf),
        "zi": pltpu.VMEM((2, hz, qb, rows, width), bf),
        "xo": pltpu.VMEM((2, hx, owned, rows, width), bf),
        "xi": pltpu.VMEM((2, hx, owned, rows, width), bf),
        "co": pltpu.VMEM((owned, rows, width), bf),
        "ci": pltpu.VMEM((owned, rows, width), bf),
        "ys_s": dma((2, hy, qb)),
        "ys_r": dma((ny, qb)),
        "zs_s": dma((2, hz, qb)),
        "zs_r": dma((nz, qb)),
        "xs_s": dma((2, hx, owned)),
        "xs_r": dma((nx, owned)),
        "cs": dma((4,)),
        "ay_s": dma((ny,)),
        "ay_r": dma((ny,)),
        "az_s": dma((nz,)),
        "az_r": dma((nz,)),
        "ty_s": dma((ny,)),
        "ty_r": dma((ny,)),
        "tz_s": dma((nz,)),
        "tz_r": dma((nz,)),
        "fz_s": dma((nz,)),
        "fz_r": dma((nz,)),
        "ry_s": dma((2, hy, qb)),
        "ry_r": dma((2, hy, qb)),
        "rz_s": dma((2, hz, qb)),
        "rz_r": dma((2, hz, qb)),
        "rx_s": dma((2, hx, owned)),
        "rx_r": dma((2, hx, owned)),
    }
    for h in range(1, nx):
        plan[f"px{h}"] = pltpu.VMEM((owned, rows, width), bf)
    return plan


def kernel(sizes, names, q_ref, p_ref, cand_ref, own_ref, pos_ref, w_ref, gq_ref, gp_ref, *scratch):
    nx, ny, nz = sizes
    s = dict(zip(names, scratch))
    qb, rows, width = q_ref.shape
    owned = p_ref.shape[0]
    ncand = cand_ref.shape[0]
    lanes = qb * rows
    scale = 3.0 / math.sqrt(width)
    dp_size = nx * ny
    g, dp = lax.axis_index("group"), lax.axis_index("dp")
    x, y = dp // ny, dp % ny
    z, c = g // CORES, g % CORES

    def at_y(r):
        return (g, x * ny + (y + r) % ny)

    def at_x(r):
        return (g, ((x + r) % nx) * ny + y)

    def at_z(r):
        return (((z + r) % nz) * CORES + c, dp)

    partner = (z * CORES + (1 - c), dp)

    tile_row = lax.broadcasted_iota(jnp.int32, (8, lanes), 0)
    w_row = jnp.concatenate([w_ref[b : b + 1, :] for b in range(qb)], axis=1) * scale
    pos_row = jnp.concatenate([pos_ref[b : b + 1, :] for b in range(qb)], axis=1).astype(jnp.float32)
    own_aux = jnp.where(tile_row == 0, w_row, jnp.where(tile_row == 1, pos_row, 0.0))
    s["auxy"][0] = own_aux
    s["auxz"][0] = own_aux

    peers = [at_y(r) for r in range(1, ny)] + [at_z(r) for r in range(1, nz)] + [partner]
    peers += [at_x(r) for r in sorted({1 % nx, (nx - 1) % nx} - {0})]
    barrier = pltpu.get_barrier_semaphore()
    for peer in peers:
        pl.semaphore_signal(barrier, inc=1, device_id=peer, device_id_type=MESH)
    pl.semaphore_wait(barrier, len(peers))

    started = []

    def send(src, dst, send_sem, recv_sem, device):
        return pltpu.make_async_remote_copy(
            src_ref=src, dst_ref=dst, send_sem=send_sem, recv_sem=recv_sem, device_id=device, device_id_type=MESH
        )

    def start(copy):
        copy.start()
        started.append(copy)

    def line_steps(n, parts, t):
        half = n // 2
        if t < half - 1:
            return [(way, part) for part in range(parts) for way in (0, 1)]
        return [(way, part) for part in range(parts) for way in (0, 1) if (part >= parts // 2) == (way == 1)]

    def slots(n, way, t):
        return ((-t) % n, (-(t + 1)) % n) if way == 0 else (t, t + 1)

    def query_copy(line, n, device_at, way, t, part):
        src, dst = slots(n, way, t)
        buf = s["q" + line]
        block = pl.ds(part * rows, rows)
        return send(
            q_ref.at[part] if t == 0 else buf.at[src, block],
            buf.at[dst, block],
            s[line + "s_s"].at[way, t, part],
            s[line + "s_r"].at[dst, part],
            device_at(1 if way == 0 else n - 1),
        )

    def y_copy(way, t, part):
        return query_copy("y", ny, at_y, way, t, part)

    def z_copy(way, t, part):
        return query_copy("z", nz, at_z, way, t, part)

    passages = [p_ref] + [s[f"px{h}"] for h in range(1, nx)] + [s["pc"]]

    def x_copy(way, t, part):
        src, dst = slots(nx, way, t)
        return send(
            passages[src].at[part],
            passages[dst].at[part],
            s["xs_s"].at[way, t, part],
            s["xs_r"].at[dst, part],
            at_x(1 if way == 0 else nx - 1),
        )

    if ny > 1:
        for way, part in line_steps(ny, qb, 0):
            start(y_copy(way, 0, part))
    if nz > 1:
        for way, part in line_steps(nz, qb, 0):
            start(z_copy(way, 0, part))
    first = sorted(line_steps(nx, owned, 0), key=lambda e: (e[1] + (owned // 2 if e[0] else 0)) % owned)
    for way, part in first:
        start(x_copy(way, 0, part))
    core_gather = send(p_ref, s["pc"], s["cs"].at[0], s["cs"].at[1], partner)
    start(core_gather)

    def spread(name, n, device_at, src, dst, sems):
        copies = [
            send(src, dst.at[n - r], s[sems + "_s"].at[r], s[sems + "_r"].at[n - r], device_at(r)) for r in range(1, n)
        ]
        for copy in copies:
            start(copy)
        return copies

    aux_y = spread("aux", ny, at_y, s["auxy"].at[0], s["auxy"], "ay")
    aux_z = spread("aux", nz, at_z, s["auxz"].at[0], s["auxz"], "az")

    def entry_y(h, r):
        return (h * ny + r) * 3

    def entry_z(h, r):
        return (nx * ny + h * nz + r) * 3

    def fill(lister, holders, entries):
        found = [jnp.int32(0)] * len(holders)
        for b in range(qb):
            listing = [jnp.int32(-1)] * len(holders)
            for k in range(ncand):
                place = own_ref[cand_ref[k, lister * qb + b]]
                for i, holder in enumerate(holders):
                    offset = place - holder * owned
                    hit = (offset >= 0) & (offset < owned)
                    listing[i] = jnp.where(hit, k, listing[i])
                    found[i] = jnp.where(hit, offset, found[i])
            for i, entry in enumerate(entries):
                s["tab"][entry + b] = listing[i]
        for i, entry in enumerate(entries):
            s["tab"][entry + 2] = found[i]

    def fill_y(r, carry):
        holders = [g * dp_size + ((x + h) % nx) * ny + y for h in range(nx)]
        fill(g * dp_size + x * ny + (y + r) % ny, holders, [entry_y(h, r) for h in range(nx)])
        return carry

    def fill_z(r, carry):
        own = jnp.where(r == 0, -1000, g * dp_size + dp)
        other = (z * CORES + (1 - c)) * dp_size + dp
        fill((((z + r) % nz) * CORES + c) * dp_size + dp, [own, other], [entry_z(h, r) for h in range(CORES)])
        return carry

    s["qy"][0] = q_ref[...].reshape(lanes, width)
    s["qz"][0] = q_ref[...].reshape(lanes, width)
    lax.fori_loop(0, nz, fill_z, 0)
    lax.fori_loop(0, ny, fill_y, 0)

    lane = lax.broadcasted_iota(jnp.int32, (1, lanes), 1)

    def listing_row(entry):
        row = jnp.full((1, lanes), s["tab"][entry], jnp.int32)
        for b in range(1, qb):
            row = jnp.where(lane >= b * rows, s["tab"][entry + b], row)
        return row

    def score(held, entry, q, index, m_ref, lse_ref, h, r):
        block = held[s["tab"][entry + 2]]
        scores = lax.dot_general(block, q, (((1,), (1,)), ((), ())), preferred_element_type=jnp.float32) * scale
        scores = jnp.where(listing_row(entry) >= 0, scores, NEG)
        top = jnp.max(scores, axis=0, keepdims=True)
        powers = jnp.exp(scores - top)
        s["e"][index] = powers
        m_ref[h, pl.ds(r, 1), :] = top
        lse_ref[h, pl.ds(r, 1), :] = top + jnp.log(jnp.sum(powers, axis=0, keepdims=True))

    def score_y(h, r):
        score(passages[h], entry_y(h, r), s["qy"][r], h * ny + r, s["my"], s["sy"], h, r)

    held_z = [p_ref, s["pc"]]

    def score_z(h, r):
        score(held_z[h], entry_z(h, r), s["qz"][r], nx * ny + h * nz + r, s["mz"], s["sz"], h, r)

    def each(count, first_slot, n, body):
        def step(i, carry):
            body((i + first_slot) % n)
            return carry

        lax.fori_loop(0, count, step, 0)

    def pass_on(t):
        for part in range(qb):
            for n, copy in ((ny, y_copy), (nz, z_copy)):
                if n > 1 and 1 <= t <= n // 2 - 1:
                    for way, piece in line_steps(n, qb, t - 1):
                        if piece == part:
                            copy(way, t - 1, part).wait_recv()
                            if (way, part) in line_steps(n, qb, t):
                                start(copy(way, t, part))

    half_y, half_z, half_x = ny // 2, nz // 2, nx // 2
    pass_on(1)
    pass_on(2)
    for t in range(1, half_x):
        for way, part in sorted(line_steps(nx, owned, t - 1), key=lambda e: (e[1] + (owned // 2 if e[0] else 0)) % owned):
            if (way, part) in line_steps(nx, owned, t):
                x_copy(way, t - 1, part).wait_recv()
                start(x_copy(way, t, part))
    core_gather.wait_recv()
    near_y, near_z = max(half_y - 2, 0), max(half_z - 2, 0)

    def near_pairs_y(r):
        score_y(0, r)

    def pairs_z(r):
        for h in range(CORES):
            score_z(h, r)

    each(2 * near_y + 1, ny - near_y, ny, near_pairs_y)
    pass_on(3)
    each(2 * near_z + 1, nz - near_z, nz, pairs_z)
    for n, copy in ((nz, z_copy), (ny, y_copy)):
        if n > 1:
            for way, part in line_steps(n, qb, n // 2 - 1):
                copy(way, n // 2 - 1, part).wait_recv()
    each(nz - 2 * near_z - 1, near_z + 1, nz, pairs_z)

    def merge(parts):
        top = functools.reduce(jnp.maximum, parts)
        return top + jnp.log(sum(jnp.exp(part - top) for part in parts))

    s["zst"][...] = merge([s["sz"][h] for h in range(CORES)])
    stat_z = spread("stat", nz, at_z, s["zst"], s["zsr"], "tz")
    each(ny - 2 * near_y - 1, near_y + 1, ny, near_pairs_y)

    for t in range(half_x):
        for way, part in line_steps(nx, owned, t):
            if t == half_x - 1 or (way, part) not in line_steps(nx, owned, t + 1):
                if t < half_x - 1:
                    x_copy(way, t, part).wait_recv()
    middle = [h for h in range(1, nx) if h != half_x]

    def side_pairs(r):
        for h in middle:
            score_y(h, r)

    if middle:
        each(ny, 0, ny, side_pairs)
    own_z = [s["zst"][0:1, :]]
    for copy in stat_z:
        copy.wait_recv()
    own_z += [s["zsr"][j][nz - j : nz - j + 1, :] for j in range(1, nz)]
    z_row = merge(own_z)
    if nx > 1:
        for way, part in line_steps(nx, owned, half_x - 1):
            x_copy(way, half_x - 1, part).wait_recv()
        each(ny, 0, ny, lambda r: score_y(half_x, r))

    stat = merge([s["sy"][h] for h in range(nx)])
    ring_row = lax.broadcasted_iota(jnp.int32, (ny, lanes), 0)
    stat = jnp.where(ring_row == 0, merge([stat, jnp.broadcast_to(z_row, stat.shape)]), stat)
    s["yst"][...] = stat
    stat_y = spread("stat", ny, at_y, s["yst"], s["ysr"], "ty")
    for copy in aux_y + aux_z:
        copy.wait_recv()
    for copy in stat_y:
        copy.wait_recv()

    def turned(value, places):
        if ny == 8:
            return pltpu.roll(value, places, axis=0)
        return jnp.concatenate([value[ny - places :], value[: ny - places]], axis=0)

    total = merge([stat] + [turned(s["ysr"][j], j) for j in range(1, ny)])
    s["ya"][...] = total
    s["fin"][...] = jnp.broadcast_to(total[0:1, :], (8, lanes))
    fin_z = spread("fin", nz, at_z, s["fin"], s["zfr"], "fz")

    down = lax.broadcasted_iota(jnp.int32, (rows, lanes), 0).astype(jnp.float32)

    def dscore(index, entry, m_row, a_row, w_line, pos_line):
        factor = jnp.exp(m_row - a_row) * w_line
        spot = pos_line - (listing_row(entry) * rows).astype(jnp.float32)
        value = s["e"][index] * factor - jnp.where(down == spot, w_line, 0.0)
        s["d"][index] = value.astype(jnp.bfloat16)

    def dscore_y(h, r):
        dscore(
            h * ny + r,
            entry_y(h, r),
            s["my"][h, pl.ds(r, 1), :],
            s["ya"][pl.ds(r, 1), :],
            s["auxy"][r, 0:1, :],
            s["auxy"][r, 1:2, :],
        )

    def dscore_z(h, r, a_row):
        dscore(
            nx * ny + h * nz + r,
            entry_z(h, r),
            s["mz"][h, pl.ds(r, 1), :],
            a_row,
            s["auxz"][r, 0:1, :],
            s["auxz"][r, 1:2, :],
        )

    def term(index, q, r):
        s["t"][r] = jnp.dot(s["d"][index], q, preferred_element_type=jnp.float32)

    strip = min(rows, 32)

    def collect(out, n, entry):
        def block(i, carry):
            p = i // (rows // strip)
            part = pl.ds((i % (rows // strip)) * strip, strip)
            acc = jnp.zeros((strip, width), jnp.float32)
            for r in range(n):
                acc += jnp.where(s["tab"][entry(r) + 2] == p, 1.0, 0.0) * s["t"][r, part, :]
            out[p, part, :] = acc.astype(out.dtype)
            return carry

        lax.fori_loop(0, owned * (rows // strip), block, 0)

    def terms_y(h, r):
        term(h * ny + r, s["qy"][r], r)

    def query_part(out, r, pairs):
        acc = None
        for index, held, entry in pairs:
            block = held[s["tab"][entry + 2]]
            part = lax.dot_general(
                s["d"][index], block, (((0,), (0,)), ((), ())), preferred_element_type=jnp.float32
            )
            acc = part if acc is None else acc + part
        out[r] = acc

    def reduce_copy(line, n, device_at, way, t, part):
        return send(
            s[line + "o"].at[way, t - 1, part],
            s[line + "i"].at[way, t - 1, part],
            s["r" + line + "_s"].at[way, t - 1, part],
            s["r" + line + "_r"].at[way, t - 1, part],
            device_at(1 if way == 0 else n - 1),
        )

    def reduce_send(line, n, device_at, way, t, part, value, alone):
        if not alone:
            reduce_copy(line, n, device_at, way, t + 1, part).wait_recv()
            value = value + s[line + "i"][way, t, part].astype(jnp.float32)
        s[line + "o"][way, t - 1, part] = value.astype(jnp.bfloat16)
        start(reduce_copy(line, n, device_at, way, t, part))

    def query_send(line, n, device_at, t, alone):
        if t < 1 or t > n // 2:
            return
        for part in range(qb):
            for way in (0, 1):
                if (way, part) not in line_steps(n, qb, t - 1):
                    continue
                first_here = t == n // 2 or (way, part) not in line_steps(n, qb, t)
                if first_here != alone:
                    continue
                target = t if way == 0 else (n - t) % n
                value = s["gq" + line][target, pl.ds(part * rows, rows), :]
                reduce_send(line, n, device_at, way, t, part, value, alone)

    def passage_send(t, alone):
        for part in range(owned):
            for way in (0, 1):
                if (way, part) not in line_steps(nx, owned, t - 1):
                    continue
                first_here = t == half_x or (way, part) not in line_steps(nx, owned, t)
                if first_here != alone:
                    continue
                target = t if way == 0 else (nx - t) % nx
                reduce_send("x", nx, at_x, way, t, part, s["gp"][target, part], alone)

    def grad_x(h):
        def both(r):
            terms_y(h, r)

        each(ny, 0, ny, both)
        collect(s["gp"].at[h], ny, lambda r: entry_y(h, r))

    if nx > 1:
        each(ny, 0, ny, lambda r: dscore_y(half_x, r))
        grad_x(half_x)
        passage_send(half_x, True)
    rest = [h for h in range(nx) if nx == 1 or h != half_x]

    def query_y(r):
        for h in rest:
            dscore_y(h, r)
        query_part(s["gqy"], r, [(h * ny + r, passages[h], entry_y(h, r)) for h in range(nx)])

    far_y = min(3, ny)
    start_y = (half_y - 1) % ny
    each(far_y, start_y, ny, query_y)
    query_send("y", ny, at_y, half_y, True)
    query_send("y", ny, at_y, half_y - 1, True)
    each(ny - far_y, (start_y + far_y) % ny, ny, query_y)
    for t in range(half_x - 1, 0, -1):
        for h in sorted({t, nx - t}):
            grad_x(h)
        passage_send(t, True)
    if half_y > 1:
        query_send("y", ny, at_y, half_y - 1, False)

    for copy in fin_z:
        copy.wait_recv()
    s["zfr"][0] = s["fin"][...]

    def query_z(r):
        a_row = s["zfr"][r, 0:1, :]
        for h in range(CORES):
            dscore_z(h, r, a_row)
        query_part(s["gqz"], r, [(nx * ny + h * nz + r, held_z[h], entry_z(h, r)) for h in range(CORES)])

    far_z = min(3, nz)
    start_z = (half_z - 1) % nz
    each(far_z, start_z, nz, query_z)
    query_send("z", nz, at_z, half_z, True)
    query_send("z", nz, at_z, half_z - 1, True)
    each(nz - far_z, (start_z + far_z) % nz, nz, query_z)
    query_send("y", ny, at_y, half_y - 2, False) if half_y > 2 else None
    if half_z > 1:
        query_send("z", nz, at_z, half_z - 1, False)

    def grad_z(h):
        each(nz, 0, nz, lambda r: term(nx * ny + h * nz + r, s["qz"][r], r))
        out = s["co"] if h == 1 else s["gp"].at[nx]
        collect(out, nz, lambda r: entry_z(h, r))

    grad_z(1)
    core_reduce = send(s["co"], s["ci"], s["cs"].at[2], s["cs"].at[3], partner)
    start(core_reduce)
    for t in range(half_x - 1, 0, -1):
        passage_send(t, False)
    for t in range(half_y - 3, 0, -1):
        query_send("y", ny, at_y, t, False)
    grad_z(0)
    grad_x(0)
    for t in range(half_z - 2, 0, -1):
        query_send("z", nz, at_z, t, False)

    def arrived(line, n, device_at, parts, part):
        total = None
        for way in (0, 1):
            if n > 1 and (way, part) in line_steps(n, parts, 0):
                reduce_copy(line, n, device_at, way, 1, part).wait_recv()
                value = s[line + "i"][way, 0, part].astype(jnp.float32)
                total = value if total is None else total + value
        return 0.0 if total is None else total

    for part in range(qb):
        block = pl.ds(part * rows, rows)
        value = s["gqy"][0, block, :] + s["gqz"][0, block, :]
        value += arrived("y", ny, at_y, qb, part)
        value += arrived("z", nz, at_z, qb, part)
        gq_ref[part] = value.astype(gq_ref.dtype)
    core_reduce.wait_recv()
    for part in range(owned):
        value = s["gp"][0, part] + s["gp"][nx, part] + s["ci"][part].astype(jnp.float32)
        value += arrived("x", nx, at_x, owned, part)
        gp_ref[part] = value.astype(gp_ref.dtype)
    for copy in started:
        copy.wait_send()


def solution(mesh, sizes=SIZES):
    nx, ny = sizes
    nz = mesh.shape["group"] // CORES
    assert mesh.shape["dp"] == nx * ny

    def shards(queries, passages, candidates, positives, row_weight, owner_map):
        plan = scratch_plan(nx, ny, nz, queries.shape[0], *passages.shape)
        vmem = pl.BlockSpec(memory_space=pltpu.VMEM)
        smem = pl.BlockSpec(memory_space=pltpu.SMEM)
        return pl.pallas_call(
            functools.partial(kernel, (nx, ny, nz), tuple(plan)),
            out_shape=(
                jax.ShapeDtypeStruct(queries.shape, queries.dtype),
                jax.ShapeDtypeStruct(passages.shape, passages.dtype),
            ),
            in_specs=[vmem, vmem, smem, smem, vmem, vmem],
            out_specs=(vmem, vmem),
            scratch_shapes=list(plan.values()),
            compiler_params=pltpu.CompilerParams(
                collective_id=0, has_side_effects=True, vmem_limit_bytes=64_000_000
            ),
        )(queries, passages, candidates.T, owner_map, positives, row_weight)

    return jax.shard_map(
        shards,
        mesh=mesh,
        in_specs=(
            P(("group", "dp"), None, None),
            P(("group", "dp"), None, None),
            P(),
            P(("group", "dp"), None),
            P(("group", "dp"), None),
            P(),
        ),
        out_specs=(P(("group", "dp"), None, None), P(("group", "dp"), None, None)),
        check_vma=False,
    )
```

time: 398 us -> 104 us (0.26); the launches traced: 394 us -> 104 us
  waiting for transfers between devices: 256 us -> 0 us
  Pallas kernels: 0 us -> 99.5 us
  other arithmetic: 47.3 us -> 0 us
  local copies, waits for them, and re-layouts: 36.5 us -> 3.77 us
  starting transfers between devices: 32.6 us -> 0 us
  matrix products: 20.1 us -> 0 us
    all_to_all x4 -> x0, waiting for transfers between devices: 256 us -> none  [the longest x1 93.9 us: shards(): lax.all_to_all(serve_blocks(asked_local, passages), 'dp', split_axis=0, c...]
    pallas_call x0 -> x1, Pallas kernels: none -> 99.5 us  [shards(): pl.pallas_call(functools.partial(kernel, (nx, ny, nz), tuple(plan)), out_...]
    all_to_all x4 -> x0, starting transfers between devices: 32.6 us -> none  [the longest x1 10.4 us: shards(): lax.all_to_all(serve_blocks(asked_remote, passages), 'group', split_axis=...]
    dot_general x6 -> x0, matrix products: 20.1 us -> none  [the longest x2 5.29 us: add_block(): jnp.einsum('rkj,rd->kjd', dscore[index], queries[index], preferred_elemen...]
    scatter-add x2 -> x0, other arithmetic: 19.5 us -> none  [add_block(): return totals.at[slot_grid[index]].add(block_terms)]
    gather x10 -> x0, local copies, waits for them, and re-layouts: 19.4 us -> none  [the longest x7 10.3 us: route_plan(): positions = jnp.take(owner_map, listed_ids)]
    convert_element_type x2 -> x0, other arithmetic: 8.92 us -> none  [the longest x1 8.16 us: shards(): slot_terms = slot_terms.astype(jnp.bfloat16)]
    reshape x2 -> x0, local copies, waits for them, and re-layouts: 7.76 us -> none  [the longest x1 4.59 us: shards(): slot_terms[:local_slots_all].reshape(dp_size, local_cap, block_rows, width)]
  transfers between devices with their start and end apart: 4 -> 0, of which waited for: 4 -> 0; matrix products, arithmetic and copies ran while one was open for 8% -> 0% of each run, Pallas kernels for 0% -> 0%
where the time goes in v1:
time: 104 us
  Pallas kernels  99.5 us (96%)
  local copies, waits for them, and re-layouts  3.77 us (4%)
    pallas_call x1, Pallas kernels, shards(): pl.pallas_call(functools.partial(kernel, (nx, ny, nz), tuple(plan)), out_...  99.5 us
    unnamed x2, local copies, waits for them, and re-layouts  3.77 us

profile of v1, /device:TPU:6, one launch (start us, length us, event | category | flops | bytes accessed | tf_op | source)
XLA Modules:
  0.0 103.9 jit_solution(8590338305818850490)
XLA Ops:
  0.6 99.5 %shard_map.77 = (bf16[2,128,512]{2,1,0:T(8,128)(2,1)}, bf16[6,128,512]{2,1,0:T(8,128)(2,1)}) custom-call(bf16[2,128,512]{2,1,0:T(8,128)(2,1)} %q_ref.1, bf16[6,128,512]{2,1,0:T(8,128)(2,1)} %p_ref.1, s32[16,1024]{1,0:T(8,128)} %bitcast.1, s32[3072]{0:T(1024)} %own_ref.1, s32[2,128]{1,0:T(2,128)} %pos_ref.1, f32[2,128]{1,0:T(2,128)} %w_ref.1), custom_call_target="tpu_custom_call" | custom-call | tf_op jit(solution)/shard_map/pallas_call | solution.py:553
  100.2 1.7 %copy.10 = bf16[2,128,512]{2,1,0:T(8,128)(2,1)} copy(bf16[2,128,512]{2,1,0:T(8,128)(2,1)} %get-tuple-element.4) | data formatting | bytes 524288
  101.8 2.1 %copy.11 = bf16[6,128,512]{2,1,0:T(8,128)(2,1)} copy(bf16[6,128,512]{2,1,0:T(8,128)(2,1)} %get-tuple-element.5) | data formatting | bytes 1572864

commit v2 on v1

v2 whole, which is shorter than its diff:
```python
import functools
import math

import jax
import jax.numpy as jnp
from jax import lax
from jax.experimental import pallas as pl
from jax.experimental.pallas import tpu as pltpu
from jax.sharding import PartitionSpec as P

MESH = pl.DeviceIdType.MESH
NEG = -1e30
CORES = 2
SIZES = (4, 8)


def scratch_plan(nx, ny, nz, qb, owned, rows, width, cand_shape, map_shape):
    lanes = qb * rows
    dma = pltpu.SemaphoreType.DMA
    bf, f32 = jnp.bfloat16, jnp.float32
    plan = {
        "qy": pltpu.VMEM((ny, lanes, width), bf),
        "qz": pltpu.VMEM((nz, lanes, width), bf),
        "pc": pltpu.VMEM((owned, rows, width), bf),
        "tab": pltpu.SMEM(((nx * ny + CORES * nz) * 3,), jnp.int32),
        "auxy": pltpu.VMEM((ny, 8, lanes), f32),
        "auxz": pltpu.VMEM((nz, 8, lanes), f32),
        "e": pltpu.VMEM((nx * ny + CORES * nz, rows, lanes), f32),
        "d": pltpu.VMEM((nx * ny + CORES * nz, rows, lanes), bf),
        "my": pltpu.VMEM((nx, ny, lanes), f32),
        "sy": pltpu.VMEM((nx, ny, lanes), f32),
        "mz": pltpu.VMEM((CORES, nz, lanes), f32),
        "sz": pltpu.VMEM((CORES, nz, lanes), f32),
        "zst": pltpu.VMEM((nz, lanes), f32),
        "zsr": pltpu.VMEM((nz, nz, lanes), f32),
        "yst": pltpu.VMEM((ny, lanes), f32),
        "ysr": pltpu.VMEM((ny, ny, lanes), f32),
        "ya": pltpu.VMEM((ny, lanes), f32),
        "fin": pltpu.VMEM((8, lanes), f32),
        "zfr": pltpu.VMEM((nz, 8, lanes), f32),
        "gqy": pltpu.VMEM((ny, lanes, width), f32),
        "gqz": pltpu.VMEM((nz, lanes, width), f32),
        "chain": pltpu.VMEM((nx + CORES, max(ny, nz) + 1, rows, width), f32),
        "own": pltpu.VMEM((owned, rows, width), f32),
        "yo": pltpu.VMEM((max(ny - 1, 1) * qb, rows, width), bf),
        "yi": pltpu.VMEM((max(ny - 1, 1) * qb, rows, width), bf),
        "zo": pltpu.VMEM((max(nz - 1, 1) * qb, rows, width), bf),
        "zi": pltpu.VMEM((max(nz - 1, 1) * qb, rows, width), bf),
        "xo": pltpu.VMEM((max(nx - 1, 1) * owned, rows, width), bf),
        "xi": pltpu.VMEM((max(nx - 1, 1) * owned, rows, width), bf),
        "co": pltpu.VMEM((owned, rows, width), bf),
        "ci": pltpu.VMEM((owned, rows, width), bf),
        "gqo": pltpu.VMEM((qb, rows, width), bf),
        "gpo": pltpu.VMEM((owned, rows, width), bf),
        "p0": pltpu.VMEM((owned, rows, width), bf),
        "cand": pltpu.SMEM(cand_shape, jnp.int32),
        "map": pltpu.SMEM(map_shape, jnp.int32),
        "posv": pltpu.VMEM((qb, rows), jnp.int32),
        "wv": pltpu.VMEM((qb, rows), f32),
        "links": pltpu.SMEM(((nx + CORES) * (max(ny, nz) + owned),), jnp.int32),
        "sent": dma((13,)),
        "got": dma((8,)),
        "near": dma((7,)),
        "yr": dma((max(ny - 1, 1) * qb,)),
        "zr": dma((max(nz - 1, 1) * qb,)),
        "xr": dma((max(nx - 1, 1) * owned,)),
        "xr2": dma((max(nx - 1, 1) * owned,)),
    }
    for h in range(1, nx):
        plan[f"px{h}"] = pltpu.VMEM((owned, rows, width), bf)
    return plan


def kernel(sizes, names, q_ref, p_ref, cand_ref, own_ref, pos_ref, w_ref, gq_ref, gp_ref, *scratch):
    nx, ny, nz = sizes
    s = dict(zip(names, scratch))
    qb, rows, width = q_ref.shape
    owned = p_ref.shape[0]
    ncand = cand_ref.shape[0]
    lanes = qb * rows
    scale = 3.0 / math.sqrt(width)
    dp_size = nx * ny
    g, dp = lax.axis_index("group"), lax.axis_index("dp")
    x, y = dp // ny, dp % ny
    z, c = g // CORES, g % CORES

    def at_y(r):
        return (g, x * ny + (y + r) % ny)

    def at_x(r):
        return (g, ((x + r) % nx) * ny + y)

    def at_z(r):
        return (((z + r) % nz) * CORES + c, dp)

    partner = (z * CORES + (1 - c), dp)

    peers = [at_y(r) for r in range(1, ny)] + [at_z(r) for r in range(1, nz)] + [partner]
    peers += [at_x(r) for r in sorted({1 % nx, (nx - 1) % nx} - {0})]
    def fetch(src, dst, sem):
        copy = pltpu.make_async_copy(src, dst, s["near"].at[sem])
        copy.start()
        return copy

    scalars = [fetch(cand_ref, s["cand"], 0), fetch(own_ref, s["map"], 1)]
    rows_in = [fetch(pos_ref, s["posv"], 2), fetch(w_ref, s["wv"], 3)]
    barrier = pltpu.get_barrier_semaphore()
    for peer in peers:
        pl.semaphore_signal(barrier, inc=1, device_id=peer, device_id_type=MESH)
    pl.semaphore_wait(barrier, len(peers))

    def send(src, dst, family, recv_sem, device):
        return pltpu.make_async_remote_copy(
            src_ref=src,
            dst_ref=dst,
            send_sem=s["sent"].at[family],
            recv_sem=recv_sem,
            device_id=device,
            device_id_type=MESH,
        )

    def start(copy):
        copy.start()

    def all_sent(family, extent):
        send(extent, extent, family, s["got"].at[7], partner).wait_send()

    def line_steps(n, parts, t):
        half = n // 2
        if t < half - 1:
            return [(way, part) for part in range(parts) for way in (0, 1)]
        return [(way, part) for part in range(parts) for way in (0, 1) if (part >= parts // 2) == (way == 1)]

    def slots(n, way, t):
        return ((-t) % n, (-(t + 1)) % n) if way == 0 else (t, t + 1)

    def entry(n, parts, way, t, part):
        half = n // 2
        return (2 * t + way) * parts + part if t < half - 1 else 2 * (half - 1) * parts + part

    def query_copy(line, n, device_at, way, t, part):
        src, dst = slots(n, way, t)
        buf = s["q" + line]
        block = pl.ds(part * rows, rows)
        return send(
            q_ref.at[part] if t == 0 else buf.at[src, block],
            buf.at[dst, block],
            "yz".index(line),
            s[line + "r"].at[entry(n, qb, way, t, part)],
            device_at(1 if way == 0 else n - 1),
        )

    def y_copy(way, t, part):
        return query_copy("y", ny, at_y, way, t, part)

    def z_copy(way, t, part):
        return query_copy("z", nz, at_z, way, t, part)

    passages = [s["p0"]] + [s[f"px{h}"] for h in range(1, nx)]

    def x_copy(way, t, part):
        src, dst = slots(nx, way, t)
        return send(
            p_ref.at[part] if t == 0 else passages[src].at[part],
            passages[dst].at[part],
            2,
            s["xr"].at[entry(nx, owned, way, t, part)],
            at_x(1 if way == 0 else nx - 1),
        )

    if ny > 1:
        for way, part in line_steps(ny, qb, 0):
            start(y_copy(way, 0, part))
    if nz > 1:
        for way, part in line_steps(nz, qb, 0):
            start(z_copy(way, 0, part))
    first = sorted(line_steps(nx, owned, 0), key=lambda e: (e[1] + (owned // 2 if e[0] else 0)) % owned)
    for way, part in first:
        start(x_copy(way, 0, part))
    core_gather = send(p_ref, s["pc"], 3, s["got"].at[0], partner)
    start(core_gather)

    whole_q = [fetch(q_ref.at[b], s["qy"].at[0, pl.ds(b * rows, rows)], 4 + b) for b in range(qb)]
    whole_p = fetch(p_ref, s["p0"], 4 + qb)
    for copy in rows_in:
        copy.wait()
    tile_row = lax.broadcasted_iota(jnp.int32, (8, lanes), 0)
    w_row = jnp.concatenate([s["wv"][b : b + 1, :] for b in range(qb)], axis=1) * scale
    pos_row = jnp.concatenate([s["posv"][b : b + 1, :] for b in range(qb)], axis=1).astype(jnp.float32)
    own_aux = jnp.where(tile_row == 0, w_row, jnp.where(tile_row == 1, pos_row, 0.0))
    s["auxy"][0] = own_aux
    s["auxz"][0] = own_aux

    def spread(n, device_at, src, dst, family):
        for r in range(1, n):
            start(send(src, dst.at[n - r], family, s["got"].at[family - 3], device_at(r)))

        def wait():
            if n > 1:
                extent = dst.at[pl.ds(1, n - 1)]
                send(extent, extent, family, s["got"].at[family - 3], partner).wait_recv()

        return wait

    def entry_y(h, r):
        return (h * ny + r) * 3

    def entry_z(h, r):
        return (nx * ny + h * nz + r) * 3

    def fill(lister, holders, entries):
        found = [jnp.int32(0)] * len(holders)
        for b in range(qb):
            listing = [jnp.int32(-1)] * len(holders)
            for k in range(ncand):
                place = s["map"][s["cand"][k, lister * qb + b]]
                for i, holder in enumerate(holders):
                    offset = place - holder * owned
                    hit = (offset >= 0) & (offset < owned)
                    listing[i] = jnp.where(hit, k, listing[i])
                    found[i] = jnp.where(hit, offset, found[i])
            for i, entry in enumerate(entries):
                s["tab"][entry + b] = listing[i]
        for i, entry in enumerate(entries):
            s["tab"][entry + 2] = found[i]

    def fill_y(r, carry):
        holders = [g * dp_size + ((x + h) % nx) * ny + y for h in range(nx)]
        fill(g * dp_size + x * ny + (y + r) % ny, holders, [entry_y(h, r) for h in range(nx)])
        return carry

    def fill_z(r, carry):
        own = jnp.where(r == 0, -1000, g * dp_size + dp)
        other = (z * CORES + (1 - c)) * dp_size + dp
        fill((((z + r) % nz) * CORES + c) * dp_size + dp, [own, other], [entry_z(h, r) for h in range(CORES)])
        return carry

    for copy in scalars:
        copy.wait()
    lax.fori_loop(0, nz, fill_z, 0)
    for copy in whole_q:
        copy.wait()
    s["qz"][0] = s["qy"][0]
    whole_p.wait()
    aux_y = spread(ny, at_y, s["auxy"].at[0], s["auxy"], 4)
    aux_z = spread(nz, at_z, s["auxz"].at[0], s["auxz"], 5)

    lane = lax.broadcasted_iota(jnp.int32, (1, lanes), 1)

    def listing_row(entry):
        row = jnp.full((1, lanes), s["tab"][entry], jnp.int32)
        for b in range(1, qb):
            row = jnp.where(lane >= b * rows, s["tab"][entry + b], row)
        return row

    def score(pairs, q):
        blocks = [held[s["tab"][where + 2]] for held, where, _, _, _ in pairs]
        block = jnp.concatenate(blocks, axis=0) if len(blocks) > 1 else blocks[0]
        joined = lax.dot_general(block, q, (((1,), (1,)), ((), ())), preferred_element_type=jnp.float32) * scale
        for i, (_, where, index, (top_ref, lse_ref, h), r) in enumerate(pairs):
            scores = joined[i * rows : (i + 1) * rows]
            scores = jnp.where(listing_row(where) >= 0, scores, NEG)
            top = jnp.max(scores, axis=0, keepdims=True)
            powers = jnp.exp(scores - top)
            s["e"][index] = powers
            top_ref[h, pl.ds(r, 1), :] = top
            lse_ref[h, pl.ds(r, 1), :] = top + jnp.log(jnp.sum(powers, axis=0, keepdims=True))

    def score_y(hs, r):
        score([(passages[h], entry_y(h, r), h * ny + r, (s["my"], s["sy"], h), r) for h in hs], s["qy"][r])

    held_z = [s["p0"], s["pc"]]

    def score_z(r):
        pairs = [(held_z[h], entry_z(h, r), nx * ny + h * nz + r, (s["mz"], s["sz"], h), r) for h in range(CORES)]
        score(pairs, s["qz"][r])

    def each(count, first_slot, n, body):
        def step(i, carry):
            body((i + first_slot) % n)
            return carry

        lax.fori_loop(0, count, step, 0)

    def pass_on(t):
        for part in range(qb):
            for n, copy in ((ny, y_copy), (nz, z_copy)):
                if n > 1 and 1 <= t <= n // 2 - 1:
                    for way, piece in line_steps(n, qb, t - 1):
                        if piece == part:
                            copy(way, t - 1, part).wait_recv()
                            if (way, part) in line_steps(n, qb, t):
                                start(copy(way, t, part))

    half_y, half_z, half_x = ny // 2, nz // 2, nx // 2
    pass_on(1)
    lax.fori_loop(0, ny, fill_y, 0)
    pass_on(2)
    for t in range(1, half_x):
        for way, part in sorted(line_steps(nx, owned, t - 1), key=lambda e: (e[1] + (owned // 2 if e[0] else 0)) % owned):
            if (way, part) in line_steps(nx, owned, t):
                x_copy(way, t - 1, part).wait_recv()
                start(x_copy(way, t, part))
    core_gather.wait_recv()
    near_y, near_z = max(half_y - 2, 0), max(half_z - 2, 0)

    def near_pairs_y(r):
        score_y([0], r)

    span = max(ny, nz) + owned
    for h in range(nx + CORES):
        n = ny if h < nx else nz
        found = [s["tab"][(entry_y(h, r) if h < nx else entry_z(h - nx, r)) + 2] for r in range(n)]
        for r in range(n):
            before = jnp.int32(0)
            for other in range(r):
                before = jnp.where(found[other] == found[r], other + 1, before)
            s["links"][h * span + r] = before
        for p in range(owned):
            last = jnp.int32(0)
            for r in range(n):
                last = jnp.where(found[r] == p, r + 1, last)
            s["links"][h * span + max(ny, nz) + p] = last
        s["chain"][h, 0] = jnp.zeros((rows, width), jnp.float32)

    each(2 * near_y + 1, ny - near_y, ny, near_pairs_y)
    pass_on(3)
    each(2 * near_z + 1, nz - near_z, nz, score_z)
    for n, copy in ((nz, z_copy), (ny, y_copy)):
        if n > 1:
            for way, part in line_steps(n, qb, n // 2 - 1):
                copy(way, n // 2 - 1, part).wait_recv()
    each(nz - 2 * near_z - 1, near_z + 1, nz, score_z)

    def merge(parts):
        top = functools.reduce(jnp.maximum, parts)
        return top + jnp.log(sum(jnp.exp(part - top) for part in parts))

    s["zst"][...] = merge([s["sz"][h] for h in range(CORES)])
    stat_z = spread(nz, at_z, s["zst"], s["zsr"], 6)
    each(ny - 2 * near_y - 1, near_y + 1, ny, near_pairs_y)

    for t in range(half_x):
        for way, part in line_steps(nx, owned, t):
            if t == half_x - 1 or (way, part) not in line_steps(nx, owned, t + 1):
                if t < half_x - 1:
                    x_copy(way, t, part).wait_recv()
    middle = [h for h in range(1, nx) if h != half_x]

    if middle:
        each(ny, 0, ny, lambda r: score_y(middle, r))
    own_z = [s["zst"][0:1, :]]
    stat_z()
    own_z += [s["zsr"][j][nz - j : nz - j + 1, :] for j in range(1, nz)]
    z_row = merge(own_z)
    if nx > 1:
        for way, part in line_steps(nx, owned, half_x - 1):
            x_copy(way, half_x - 1, part).wait_recv()

        def last_pairs(i):
            score_y([half_x], i)
            score_y([half_x], i + ny // 2)

        each(ny // 2, 0, ny, last_pairs)

    stat = merge([s["sy"][h] for h in range(nx)])
    ring_row = lax.broadcasted_iota(jnp.int32, (ny, lanes), 0)
    stat = jnp.where(ring_row == 0, merge([stat, jnp.broadcast_to(z_row, stat.shape)]), stat)
    s["yst"][...] = stat
    stat_y = spread(ny, at_y, s["yst"], s["ysr"], 7)
    aux_y()
    aux_z()
    stat_y()

    def turned(value, places):
        if ny == 8:
            return pltpu.roll(value, places, axis=0)
        return jnp.concatenate([value[ny - places :], value[: ny - places]], axis=0)

    total = merge([stat] + [turned(s["ysr"][j], j) for j in range(1, ny)])
    s["ya"][...] = total
    s["fin"][...] = jnp.broadcast_to(total[0:1, :], (8, lanes))
    fin_z = spread(nz, at_z, s["fin"], s["zfr"], 8)

    down = lax.broadcasted_iota(jnp.int32, (rows, lanes), 0).astype(jnp.float32)

    def dscore(index, entry, m_row, a_row, w_line, pos_line):
        factor = jnp.exp(m_row - a_row) * w_line
        spot = pos_line - (listing_row(entry) * rows).astype(jnp.float32)
        value = s["e"][index] * factor - jnp.where(down == spot, w_line, 0.0)
        s["d"][index] = value.astype(jnp.bfloat16)

    def dscore_y(h, r):
        dscore(
            h * ny + r,
            entry_y(h, r),
            s["my"][h, pl.ds(r, 1), :],
            s["ya"][pl.ds(r, 1), :],
            s["auxy"][r, 0:1, :],
            s["auxy"][r, 1:2, :],
        )

    def dscore_z(h, r, a_row):
        dscore(
            nx * ny + h * nz + r,
            entry_z(h, r),
            s["mz"][h, pl.ds(r, 1), :],
            a_row,
            s["auxz"][r, 0:1, :],
            s["auxz"][r, 1:2, :],
        )

    def term(h, r, index, q):
        value = jnp.dot(s["d"][index], q, preferred_element_type=jnp.float32)
        s["chain"][h, r + 1] = value + s["chain"][h, s["links"][h * span + r]]

    def block_sum(h, p):
        return s["chain"][h, s["links"][h * span + max(ny, nz) + p]]

    def query_part(out, r, pairs):
        left = jnp.concatenate([s["d"][index] for index, _, _ in pairs], axis=0)
        right = jnp.concatenate([held[s["tab"][where + 2]] for _, held, where in pairs], axis=0)
        out[r] = lax.dot_general(left, right, (((0,), (0,)), ((), ())), preferred_element_type=jnp.float32)

    def reduce_copy(line, n, device_at, way, t, part):
        place = entry(n, owned if line == "x" else qb, way, t - 1, part)
        return send(
            s[line + "o"].at[place],
            s[line + "i"].at[place],
            9 + "yzx".index(line),
            s["xr2" if line == "x" else line + "r"].at[place],
            device_at(1 if way == 0 else n - 1),
        )

    def came(line, n, way, t, part):
        return s[line + "i"][entry(n, owned if line == "x" else qb, way, t - 1, part)].astype(jnp.float32)

    def reduce_send(line, n, device_at, way, t, part, value, alone):
        if not alone:
            reduce_copy(line, n, device_at, way, t + 1, part).wait_recv()
            value = value + came(line, n, way, t + 1, part)
        s[line + "o"][entry(n, owned if line == "x" else qb, way, t - 1, part)] = value.astype(jnp.bfloat16)
        start(reduce_copy(line, n, device_at, way, t, part))

    def query_send(line, n, device_at, t, alone):
        if t < 1 or t > n // 2:
            return
        for part in range(qb):
            for way in (0, 1):
                if (way, part) not in line_steps(n, qb, t - 1):
                    continue
                first_here = t == n // 2 or (way, part) not in line_steps(n, qb, t)
                if first_here != alone:
                    continue
                target = t if way == 0 else (n - t) % n
                value = s["gq" + line][target, pl.ds(part * rows, rows), :]
                reduce_send(line, n, device_at, way, t, part, value, alone)

    def passage_send(t, alone):
        for part in range(owned):
            for way in (0, 1):
                if (way, part) not in line_steps(nx, owned, t - 1):
                    continue
                first_here = t == half_x or (way, part) not in line_steps(nx, owned, t)
                if first_here != alone:
                    continue
                target = t if way == 0 else (nx - t) % nx
                reduce_send("x", nx, at_x, way, t, part, block_sum(target, part), alone)

    def grad_x(h):
        each(ny, 0, ny, lambda r: term(h, r, h * ny + r, s["qy"][r]))

    if nx > 1:

        def first_terms(r):
            dscore_y(half_x, r)
            term(half_x, r, half_x * ny + r, s["qy"][r])

        each(ny, 0, ny, first_terms)
        passage_send(half_x, True)
    rest = [h for h in range(nx) if nx == 1 or h != half_x]

    def query_y(r):
        for h in rest:
            dscore_y(h, r)
        query_part(s["gqy"], r, [(h * ny + r, passages[h], entry_y(h, r)) for h in range(nx)])

    far_y = min(3, ny)
    start_y = (half_y - 1) % ny
    each(far_y, start_y, ny, query_y)
    query_send("y", ny, at_y, half_y, True)
    query_send("y", ny, at_y, half_y - 1, True)
    each(ny - far_y, (start_y + far_y) % ny, ny, query_y)
    for t in range(half_x - 1, 0, -1):
        for h in sorted({t, nx - t}):
            grad_x(h)
        passage_send(t, True)
    if half_y > 1:
        query_send("y", ny, at_y, half_y - 1, False)
    fin_z()
    s["zfr"][0] = s["fin"][...]

    def query_z(r):
        a_row = s["zfr"][r, 0:1, :]
        for h in range(CORES):
            dscore_z(h, r, a_row)
        query_part(s["gqz"], r, [(nx * ny + h * nz + r, held_z[h], entry_z(h, r)) for h in range(CORES)])

    far_z = min(3, nz)
    start_z = (half_z - 1) % nz
    each(far_z, start_z, nz, query_z)
    query_send("z", nz, at_z, half_z, True)
    query_send("z", nz, at_z, half_z - 1, True)
    each(nz - far_z, (start_z + far_z) % nz, nz, query_z)
    query_send("y", ny, at_y, half_y - 2, False) if half_y > 2 else None
    if half_z > 1:
        query_send("z", nz, at_z, half_z - 1, False)

    def grad_z(h):
        each(nz, 0, nz, lambda r: term(nx + h, r, nx * ny + h * nz + r, s["qz"][r]))

    for t in range(half_x - 1, 0, -1):
        passage_send(t, False)
    grad_z(1)
    for part in range(owned):
        s["co"][part] = block_sum(nx + 1, part).astype(jnp.bfloat16)
    core_reduce = send(s["co"], s["ci"], 12, s["got"].at[6], partner)
    start(core_reduce)
    for t in range(half_y - 3, 0, -1):
        query_send("y", ny, at_y, t, False)
    grad_z(0)
    grad_x(0)
    for t in range(half_z - 2, 0, -1):
        query_send("z", nz, at_z, t, False)

    def arrived(line, n, device_at, parts, part):
        total = None
        for way in (0, 1):
            if n > 1 and (way, part) in line_steps(n, parts, 0):
                reduce_copy(line, n, device_at, way, 1, part).wait_recv()
                value = came(line, n, way, 1, part)
                total = value if total is None else total + value
        return 0.0 if total is None else total

    core_reduce.wait_recv()
    for part in range(owned):
        s["own"][part] = block_sum(0, part) + block_sum(nx, part) + s["ci"][part].astype(jnp.float32)
    results = []
    for part in range(qb):
        block = pl.ds(part * rows, rows)
        value = s["gqy"][0, block, :] + s["gqz"][0, block, :]
        value += arrived("y", ny, at_y, qb, part)
        value += arrived("z", nz, at_z, qb, part)
        s["gqo"][part] = value.astype(gq_ref.dtype)
    results.append(fetch(s["gqo"], gq_ref, 0))
    for part in range(owned):
        value = s["own"][part] + arrived("x", nx, at_x, owned, part)
        s["gpo"][part] = value.astype(gp_ref.dtype)
    results.append(fetch(s["gpo"], gp_ref, 1))
    if ny > 1:
        for family, extent in ((0, s["yo"]), (9, s["yo"]), (4, s["auxy"].at[pl.ds(1, ny - 1)]), (7, s["ysr"].at[pl.ds(1, ny - 1)])):
            all_sent(family, extent)
    if nz > 1:
        for family, extent in ((1, s["zo"]), (10, s["zo"]), (5, s["auxz"].at[pl.ds(1, nz - 1)])):
            all_sent(family, extent)
        for family, extent in ((6, s["zsr"].at[pl.ds(1, nz - 1)]), (8, s["zfr"].at[pl.ds(1, nz - 1)])):
            all_sent(family, extent)
    if nx > 1:
        all_sent(2, s["xo"])
        all_sent(11, s["xo"])
    all_sent(3, s["pc"])
    all_sent(12, s["co"])
    for copy in results:
        copy.wait()


def hand_over(gq_in, gp_in, gq_out, gp_out, gq, gp, sems):
    pieces = [(gq_in, gq, gq_out, 0)] + [(gp_in, gp, gp_out, part) for part in range(gp_in.shape[0])]
    loads, stores = [], []
    for i, (src, held, dst, part) in enumerate(pieces):
        piece = slice(None) if i == 0 else pl.ds(part, 1)
        loads.append(pltpu.make_async_copy(src.at[piece], held.at[piece], sems.at[0, i]))
        stores.append(pltpu.make_async_copy(held.at[piece], dst.at[piece], sems.at[1, i]))
    for load in loads:
        load.start()
    for load, store in zip(loads, stores):
        load.wait()
        store.start()
    for store in stores:
        store.wait()


def solution(mesh, sizes=SIZES):
    nx, ny = sizes
    nz = mesh.shape["group"] // CORES
    assert mesh.shape["dp"] == nx * ny

    def shards(queries, passages, candidates, positives, row_weight, owner_map):
        listed = candidates.T
        plan = scratch_plan(nx, ny, nz, queries.shape[0], *passages.shape, listed.shape, owner_map.shape)
        left = pl.BlockSpec(memory_space=pl.ANY)
        shapes = (
            jax.ShapeDtypeStruct(queries.shape, queries.dtype),
            jax.ShapeDtypeStruct(passages.shape, passages.dtype),
        )
        results = pl.pallas_call(
            functools.partial(kernel, (nx, ny, nz), tuple(plan)),
            out_shape=shapes,
            in_specs=[left] * 6,
            out_specs=(left, left),
            scratch_shapes=list(plan.values()),
            compiler_params=pltpu.CompilerParams(
                collective_id=0, has_side_effects=True, vmem_limit_bytes=64_000_000
            ),
        )(queries, passages, listed, owner_map, positives, row_weight)
        return pl.pallas_call(
            hand_over,
            out_shape=shapes,
            in_specs=[left] * 2,
            out_specs=(left, left),
            scratch_shapes=[
                pltpu.VMEM(queries.shape, queries.dtype),
                pltpu.VMEM(passages.shape, passages.dtype),
                pltpu.SemaphoreType.DMA((2, passages.shape[0] + 1)),
            ],
        )(*results)

    return jax.shard_map(
        shards,
        mesh=mesh,
        in_specs=(
            P(("group", "dp"), None, None),
            P(("group", "dp"), None, None),
            P(),
            P(("group", "dp"), None),
            P(("group", "dp"), None),
            P(),
        ),
        out_specs=(P(("group", "dp"), None, None), P(("group", "dp"), None, None)),
        check_vma=False,
    )
```

time: 104 us -> 90.7 us (0.87)
  Pallas kernels: 99.5 us -> 89.8 us
  local copies, waits for them, and re-layouts: 3.77 us -> 0 us
    pallas_call x1, Pallas kernels: 99.5 us -> 87.8 us  [shards(): pl.pallas_call(functools.partial(kernel, (nx, ny, nz), tuple(plan)), out_...]
    unnamed x2 -> x0, local copies, waits for them, and re-layouts: 3.77 us -> none
    pallas_call x0 -> x1, Pallas kernels: none -> 2.03 us  [shards(): pl.pallas_call(hand_over, out_shape=shapes, in_specs=[left] * 2, out_spec...]
where the time goes in v2:
time: 90.7 us; the launch traced here: 90.5 us
  Pallas kernels  89.8 us (99%)
    pallas_call x1, Pallas kernels, shards(): pl.pallas_call(functools.partial(kernel, (nx, ny, nz), tuple(plan)), out_...  87.8 us
    pallas_call x1, Pallas kernels, shards(): pl.pallas_call(hand_over, out_shape=shapes, in_specs=[left] * 2, out_spec...  2.03 us

profile of v2, /device:TPU:6, one launch (start us, length us, event | category | flops | bytes accessed | tf_op | source)
XLA Modules:
  0.0 90.5 jit_solution(1177286931690848103)
XLA Ops:
  0.6 87.8 %shard_map.77 = (bf16[2,128,512]{2,1,0:T(8,128)(2,1)}, bf16[6,128,512]{2,1,0:T(8,128)(2,1)}) custom-call(bf16[2,128,512]{2,1,0:T(8,128)(2,1)} %q_ref.1, bf16[6,128,512]{2,1,0:T(8,128)(2,1)} %p_ref.1, s32[16,1024]{1,0:T(8,128)} %bitcast.1, s32[3072]{0:T(1024)} %own_ref.1, s32[2,128]{1,0:T(2,128)} %pos_ref.1, f32[2,128]{1,0:T(2,128)} %w_ref.1), custom_call_target="tpu_custom_call" | custom-call | tf_op jit(solution)/shard_map/pallas_call | solution.py:606
  88.5 2.0 %shard_map.78 = (bf16[2,128,512]{2,1,0:T(8,128)(2,1)}, bf16[6,128,512]{2,1,0:T(8,128)(2,1)}) custom-call(bf16[2,128,512]{2,1,0:T(8,128)(2,1)} %get-tuple-element.4.gq_in, bf16[6,128,512]{2,1,0:T(8,128)(2,1)} %get-tuple-element.5.gp_in), custom_call_target="tpu_custom_call" | custom-call | tf_op jit(solution)/shard_map/pallas_call | solution.py:616

commit v3 on v2

--- a/solution.py
+++ b/solution.py
@@ -125,11 +125,16 @@
     def all_sent(family, extent):
         send(extent, extent, family, s["got"].at[7], partner).wait_send()
 
-    def line_steps(n, parts, t):
-        half = n // 2
-        if t < half - 1:
-            return [(way, part) for part in range(parts) for way in (0, 1)]
-        return [(way, part) for part in range(parts) for way in (0, 1) if (part >= parts // 2) == (way == 1)]
+    def stream(kind, parts):
+        return [
+            (way, part)
+            for part in range(parts)
+            for way in (0, 1)
+            if ((part >= parts // 2) == (way == 1)) == (kind == "A")
+        ]
+
+    def steps(n, kind):
+        return n // 2 - (kind == "B")
 
     def slots(n, way, t):
         return ((-t) % n, (-(t + 1)) % n) if way == 0 else (t, t + 1)
@@ -168,15 +173,27 @@
             at_x(1 if way == 0 else nx - 1),
         )
 
-    if ny > 1:
-        for way, part in line_steps(ny, qb, 0):
-            start(y_copy(way, 0, part))
-    if nz > 1:
-        for way, part in line_steps(nz, qb, 0):
-            start(z_copy(way, 0, part))
-    first = sorted(line_steps(nx, owned, 0), key=lambda e: (e[1] + (owned // 2 if e[0] else 0)) % owned)
-    for way, part in first:
-        start(x_copy(way, 0, part))
+    rings = {"y": (ny, y_copy, qb), "z": (nz, z_copy, qb), "x": (nx, x_copy, owned)}
+
+    def launch(line, kind, t):
+        n, copy, parts = rings[line]
+        if t < steps(n, kind):
+            for way, part in stream(kind, parts):
+                start(copy(way, t, part))
+
+    def land(line, kind, t):
+        n, copy, parts = rings[line]
+        if t < steps(n, kind):
+            for way, part in stream(kind, parts):
+                copy(way, t, part).wait_recv()
+
+    def relay(kind, t):
+        for line in "yz":
+            land(line, kind, t - 1)
+            launch(line, kind, t)
+
+    for line in "yzx":
+        launch(line, "A", 0)
     core_gather = send(p_ref, s["pc"], 3, s["got"].at[0], partner)
     start(core_gather)
 
@@ -216,7 +233,7 @@
                 place = s["map"][s["cand"][k, lister * qb + b]]
                 for i, holder in enumerate(holders):
                     offset = place - holder * owned
-                    hit = (offset >= 0) & (offset < owned)
+                    hit = offset.astype(jnp.uint32) < jnp.uint32(owned)
                     listing[i] = jnp.where(hit, k, listing[i])
                     found[i] = jnp.where(hit, offset, found[i])
             for i, entry in enumerate(entries):
@@ -238,6 +255,8 @@
     for copy in scalars:
         copy.wait()
     lax.fori_loop(0, nz, fill_z, 0)
+    for line in "yz":
+        launch(line, "B", 0)
     for copy in whole_q:
         copy.wait()
     s["qz"][0] = s["qy"][0]
@@ -282,30 +301,17 @@
 
         lax.fori_loop(0, count, step, 0)
 
-    def pass_on(t):
-        for part in range(qb):
-            for n, copy in ((ny, y_copy), (nz, z_copy)):
-                if n > 1 and 1 <= t <= n // 2 - 1:
-                    for way, piece in line_steps(n, qb, t - 1):
-                        if piece == part:
-                            copy(way, t - 1, part).wait_recv()
-                            if (way, part) in line_steps(n, qb, t):
-                                start(copy(way, t, part))
-
     half_y, half_z, half_x = ny // 2, nz // 2, nx // 2
-    pass_on(1)
-    lax.fori_loop(0, ny, fill_y, 0)
-    pass_on(2)
+    near_y, near_z = max(half_y - 2, 0), max(half_z - 2, 0)
+    relay("A", 1)
+    lax.fori_loop(0, ny // 2, fill_y, 0)
+    relay("B", 1)
+    launch("x", "B", 0)
+    lax.fori_loop(ny // 2, ny, fill_y, 0)
+    relay("A", 2)
     for t in range(1, half_x):
-        for way, part in sorted(line_steps(nx, owned, t - 1), key=lambda e: (e[1] + (owned // 2 if e[0] else 0)) % owned):
-            if (way, part) in line_steps(nx, owned, t):
-                x_copy(way, t - 1, part).wait_recv()
-                start(x_copy(way, t, part))
-    core_gather.wait_recv()
-    near_y, near_z = max(half_y - 2, 0), max(half_z - 2, 0)
-
-    def near_pairs_y(r):
-        score_y([0], r)
+        land("x", "A", t - 1)
+        launch("x", "A", t)
 
     span = max(ny, nz) + owned
     for h in range(nx + CORES):
@@ -323,13 +329,13 @@
             s["links"][h * span + max(ny, nz) + p] = last
         s["chain"][h, 0] = jnp.zeros((rows, width), jnp.float32)
 
-    each(2 * near_y + 1, ny - near_y, ny, near_pairs_y)
-    pass_on(3)
+    relay("B", 2)
+    core_gather.wait_recv()
     each(2 * near_z + 1, nz - near_z, nz, score_z)
-    for n, copy in ((nz, z_copy), (ny, y_copy)):
-        if n > 1:
-            for way, part in line_steps(n, qb, n // 2 - 1):
-                copy(way, n // 2 - 1, part).wait_recv()
+    relay("A", 3)
+    each(2 * near_y + 1, ny - near_y, ny, lambda r: score_y([0], r))
+    relay("B", 3)
+    relay("A", 4)
     each(nz - 2 * near_z - 1, near_z + 1, nz, score_z)
 
     def merge(parts):
@@ -338,13 +344,10 @@
 
     s["zst"][...] = merge([s["sz"][h] for h in range(CORES)])
     stat_z = spread(nz, at_z, s["zst"], s["zsr"], 6)
-    each(ny - 2 * near_y - 1, near_y + 1, ny, near_pairs_y)
-
-    for t in range(half_x):
-        for way, part in line_steps(nx, owned, t):
-            if t == half_x - 1 or (way, part) not in line_steps(nx, owned, t + 1):
-                if t < half_x - 1:
-                    x_copy(way, t, part).wait_recv()
+    each(ny - 2 * near_y - 1, near_y + 1, ny, lambda r: score_y([0], r))
+
+    for t in range(half_x - 1):
+        land("x", "B", t)
     middle = [h for h in range(1, nx) if h != half_x]
 
     if middle:
@@ -354,8 +357,7 @@
     own_z += [s["zsr"][j][nz - j : nz - j + 1, :] for j in range(1, nz)]
     z_row = merge(own_z)
     if nx > 1:
-        for way, part in line_steps(nx, owned, half_x - 1):
-            x_copy(way, half_x - 1, part).wait_recv()
+        land("x", "A", half_x - 1)
 
         def last_pairs(i):
             score_y([half_x], i)
@@ -442,63 +444,40 @@
         s[line + "o"][entry(n, owned if line == "x" else qb, way, t - 1, part)] = value.astype(jnp.bfloat16)
         start(reduce_copy(line, n, device_at, way, t, part))
 
-    def query_send(line, n, device_at, t, alone):
-        if t < 1 or t > n // 2:
-            return
-        for part in range(qb):
-            for way in (0, 1):
-                if (way, part) not in line_steps(n, qb, t - 1):
-                    continue
-                first_here = t == n // 2 or (way, part) not in line_steps(n, qb, t)
-                if first_here != alone:
-                    continue
+    def query_send(line, kind, t):
+        n, device_at = (ny, at_y) if line == "y" else (nz, at_z)
+        if 1 <= t <= steps(n, kind):
+            for way, part in stream(kind, qb):
                 target = t if way == 0 else (n - t) % n
                 value = s["gq" + line][target, pl.ds(part * rows, rows), :]
-                reduce_send(line, n, device_at, way, t, part, value, alone)
-
-    def passage_send(t, alone):
-        for part in range(owned):
-            for way in (0, 1):
-                if (way, part) not in line_steps(nx, owned, t - 1):
-                    continue
-                first_here = t == half_x or (way, part) not in line_steps(nx, owned, t)
-                if first_here != alone:
-                    continue
+                reduce_send(line, n, device_at, way, t, part, value, t == steps(n, kind))
+
+    def passage_send(kind, t):
+        if 1 <= t <= steps(nx, kind):
+            for way, part in stream(kind, owned):
                 target = t if way == 0 else (nx - t) % nx
-                reduce_send("x", nx, at_x, way, t, part, block_sum(target, part), alone)
-
-    def grad_x(h):
-        each(ny, 0, ny, lambda r: term(h, r, h * ny + r, s["qy"][r]))
+                reduce_send("x", nx, at_x, way, t, part, block_sum(target, part), t == steps(nx, kind))
+
+    def grad_x(h, fresh):
+        def pair(r):
+            if fresh:
+                dscore_y(h, r)
+            term(h, r, h * ny + r, s["qy"][r])
+
+        each(ny, 0, ny, pair)
 
     if nx > 1:
-
-        def first_terms(r):
-            dscore_y(half_x, r)
-            term(half_x, r, half_x * ny + r, s["qy"][r])
-
-        each(ny, 0, ny, first_terms)
-        passage_send(half_x, True)
+        grad_x(half_x, True)
+        passage_send("A", half_x)
     rest = [h for h in range(nx) if nx == 1 or h != half_x]
 
-    def query_y(r):
-        for h in rest:
-            dscore_y(h, r)
-        query_part(s["gqy"], r, [(h * ny + r, passages[h], entry_y(h, r)) for h in range(nx)])
-
-    far_y = min(3, ny)
-    start_y = (half_y - 1) % ny
-    each(far_y, start_y, ny, query_y)
-    query_send("y", ny, at_y, half_y, True)
-    query_send("y", ny, at_y, half_y - 1, True)
-    each(ny - far_y, (start_y + far_y) % ny, ny, query_y)
-    for t in range(half_x - 1, 0, -1):
-        for h in sorted({t, nx - t}):
-            grad_x(h)
-        passage_send(t, True)
-    if half_y > 1:
-        query_send("y", ny, at_y, half_y - 1, False)
-    fin_z()
-    s["zfr"][0] = s["fin"][...]
+    def query_y(hs):
+        def body(r):
+            for h in hs:
+                dscore_y(h, r)
+            query_part(s["gqy"], r, [(h * ny + r, passages[h], entry_y(h, r)) for h in range(nx)])
+
+        return body
 
     def query_z(r):
         a_row = s["zfr"][r, 0:1, :]
@@ -506,37 +485,65 @@
             dscore_z(h, r, a_row)
         query_part(s["gqz"], r, [(nx * ny + h * nz + r, held_z[h], entry_z(h, r)) for h in range(CORES)])
 
-    far_z = min(3, nz)
-    start_z = (half_z - 1) % nz
-    each(far_z, start_z, nz, query_z)
-    query_send("z", nz, at_z, half_z, True)
-    query_send("z", nz, at_z, half_z - 1, True)
-    each(nz - far_z, (start_z + far_z) % nz, nz, query_z)
-    query_send("y", ny, at_y, half_y - 2, False) if half_y > 2 else None
-    if half_z > 1:
-        query_send("z", nz, at_z, half_z - 1, False)
-
     def grad_z(h):
         each(nz, 0, nz, lambda r: term(nx + h, r, nx * ny + h * nz + r, s["qz"][r]))
 
+    def targets(n, body, group):
+        half = n // 2
+        if group == 0:
+            each(1, half, n, body)
+        elif group == 3 and n > 1:
+            each(min(3, n - 1), n - 1 if n > 2 else 0, n, body)
+        elif group in (1, 2) and n > 2:
+            each(2, 0, 2, lambda i: body(half - group + 2 * group * i))
+
+    assert ny in (1, 2, 8) and nz in (1, 2, 8)
+    targets(ny, query_y(rest), 0)
+    query_send("y", "A", half_y)
+    for h in middle[:1]:
+        grad_x(h, True)
+    rest = [h for h in rest if h not in middle[:1]]
+    targets(ny, query_y(rest), 1)
+    query_send("y", "B", half_y - 1)
+    for h in middle[1:]:
+        grad_x(h, True)
+    rest = [h for h in rest if h not in middle]
+    targets(ny, query_y(rest), 2)
+    fin_z()
+    s["zfr"][0] = s["fin"][...]
+    targets(nz, query_z, 0)
+    query_send("z", "A", half_z)
+    query_send("y", "A", half_y - 1)
+    targets(nz, query_z, 1)
+    query_send("z", "B", half_z - 1)
     for t in range(half_x - 1, 0, -1):
-        passage_send(t, False)
+        passage_send("B", t)
+    targets(ny, query_y(rest), 3)
+    query_send("y", "B", half_y - 2)
+    targets(nz, query_z, 2)
+    targets(nz, query_z, 3)
+    query_send("z", "A", half_z - 1)
+    query_send("y", "A", half_y - 2)
+    query_send("z", "B", half_z - 2)
     grad_z(1)
     for part in range(owned):
         s["co"][part] = block_sum(nx + 1, part).astype(jnp.bfloat16)
     core_reduce = send(s["co"], s["ci"], 12, s["got"].at[6], partner)
     start(core_reduce)
-    for t in range(half_y - 3, 0, -1):
-        query_send("y", ny, at_y, t, False)
+    query_send("y", "B", half_y - 3)
+    for t in range(half_x - 1, 0, -1):
+        passage_send("A", t)
+    query_send("z", "A", half_z - 2)
+    query_send("y", "A", half_y - 3)
+    query_send("z", "B", half_z - 3)
     grad_z(0)
-    grad_x(0)
-    for t in range(half_z - 2, 0, -1):
-        query_send("z", nz, at_z, t, False)
+    grad_x(0, False)
+    query_send("z", "A", half_z - 3)
 
     def arrived(line, n, device_at, parts, part):
         total = None
         for way in (0, 1):
-            if n > 1 and (way, part) in line_steps(n, parts, 0):
+            if n > 2 or (n == 2 and (way, part) in stream("A", parts)):
                 reduce_copy(line, n, device_at, way, 1, part).wait_recv()
                 value = came(line, n, way, 1, part)
                 total = value if total is None else total + value
@@ -556,7 +563,7 @@
     for part in range(owned):
         value = s["own"][part] + arrived("x", nx, at_x, owned, part)
         s["gpo"][part] = value.astype(gp_ref.dtype)
-    results.append(fetch(s["gpo"], gp_ref, 1))
+        results.append(fetch(s["gpo"].at[part], gp_ref.at[part], 1 + part))
     if ny > 1:
         for family, extent in ((0, s["yo"]), (9, s["yo"]), (4, s["auxy"].at[pl.ds(1, ny - 1)]), (7, s["ysr"].at[pl.ds(1, ny - 1)])):
             all_sent(family, extent)

time: 90.7 us -> 84.2 us (0.928)
  Pallas kernels: 89.8 us -> 83.3 us
    pallas_call x1, Pallas kernels: 87.8 us -> 81.3 us  [shards(): pl.pallas_call(functools.partial(kernel, (nx, ny, nz), tuple(plan)), out_...]
where the time goes in v3:
time: 84.2 us; the launch traced here: 83.9 us
  Pallas kernels  83.3 us (99%)
    pallas_call x1, Pallas kernels, shards(): pl.pallas_call(functools.partial(kernel, (nx, ny, nz), tuple(plan)), out_...  81.3 us
    pallas_call x1, Pallas kernels, shards(): pl.pallas_call(hand_over, out_shape=shapes, in_specs=[left] * 2, out_spec...  2.03 us

profile of v3, /device:TPU:6, one launch (start us, length us, event | category | flops | bytes accessed | tf_op | source)
XLA Modules:
  0.0 83.9 jit_solution(733648158773185252)
XLA Ops:
  0.6 81.3 %shard_map.77 = (bf16[2,128,512]{2,1,0:T(8,128)(2,1)}, bf16[6,128,512]{2,1,0:T(8,128)(2,1)}) custom-call(bf16[2,128,512]{2,1,0:T(8,128)(2,1)} %q_ref.1, bf16[6,128,512]{2,1,0:T(8,128)(2,1)} %p_ref.1, s32[16,1024]{1,0:T(8,128)} %bitcast.1, s32[3072]{0:T(1024)} %own_ref.1, s32[2,128]{1,0:T(2,128)} %pos_ref.1, f32[2,128]{1,0:T(2,128)} %w_ref.1), custom_call_target="tpu_custom_call" | custom-call | tf_op jit(solution)/shard_map/pallas_call | solution.py:613
  81.9 2.0 %shard_map.78 = (bf16[2,128,512]{2,1,0:T(8,128)(2,1)}, bf16[6,128,512]{2,1,0:T(8,128)(2,1)}) custom-call(bf16[2,128,512]{2,1,0:T(8,128)(2,1)} %get-tuple-element.4.gq_in, bf16[6,128,512]{2,1,0:T(8,128)(2,1)} %get-tuple-element.5.gp_in), custom_call_target="tpu_custom_call" | custom-call | tf_op jit(solution)/shard_map/pallas_call | solution.py:623

commit v4 on v3

--- a/solution.py
+++ b/solution.py
@@ -11,11 +11,12 @@
 MESH = pl.DeviceIdType.MESH
 NEG = -1e30
 CORES = 2
+CUTS = 2
 SIZES = (4, 8)
 
 
 def scratch_plan(nx, ny, nz, qb, owned, rows, width, cand_shape, map_shape):
-    lanes = qb * rows
+    lanes, qp = qb * rows, qb * CUTS
     dma = pltpu.SemaphoreType.DMA
     bf, f32 = jnp.bfloat16, jnp.float32
     plan = {
@@ -23,8 +24,6 @@
         "qz": pltpu.VMEM((nz, lanes, width), bf),
         "pc": pltpu.VMEM((owned, rows, width), bf),
         "tab": pltpu.SMEM(((nx * ny + CORES * nz) * 3,), jnp.int32),
-        "auxy": pltpu.VMEM((ny, 8, lanes), f32),
-        "auxz": pltpu.VMEM((nz, 8, lanes), f32),
         "e": pltpu.VMEM((nx * ny + CORES * nz, rows, lanes), f32),
         "d": pltpu.VMEM((nx * ny + CORES * nz, rows, lanes), bf),
         "my": pltpu.VMEM((nx, ny, lanes), f32),
@@ -33,8 +32,8 @@
         "sz": pltpu.VMEM((CORES, nz, lanes), f32),
         "zst": pltpu.VMEM((nz, lanes), f32),
         "zsr": pltpu.VMEM((nz, nz, lanes), f32),
-        "yst": pltpu.VMEM((ny, lanes), f32),
-        "ysr": pltpu.VMEM((ny, ny, lanes), f32),
+        "yst": pltpu.VMEM((ny + 8, lanes), f32),
+        "ysr": pltpu.VMEM((ny, ny + 8, lanes), f32),
         "ya": pltpu.VMEM((ny, lanes), f32),
         "fin": pltpu.VMEM((8, lanes), f32),
         "zfr": pltpu.VMEM((nz, 8, lanes), f32),
@@ -42,10 +41,10 @@
         "gqz": pltpu.VMEM((nz, lanes, width), f32),
         "chain": pltpu.VMEM((nx + CORES, max(ny, nz) + 1, rows, width), f32),
         "own": pltpu.VMEM((owned, rows, width), f32),
-        "yo": pltpu.VMEM((max(ny - 1, 1) * qb, rows, width), bf),
-        "yi": pltpu.VMEM((max(ny - 1, 1) * qb, rows, width), bf),
-        "zo": pltpu.VMEM((max(nz - 1, 1) * qb, rows, width), bf),
-        "zi": pltpu.VMEM((max(nz - 1, 1) * qb, rows, width), bf),
+        "yo": pltpu.VMEM((max(ny - 1, 1) * qp, lanes // qp, width), bf),
+        "yi": pltpu.VMEM((max(ny - 1, 1) * qp, lanes // qp, width), bf),
+        "zo": pltpu.VMEM((max(nz - 1, 1) * qp, lanes // qp, width), bf),
+        "zi": pltpu.VMEM((max(nz - 1, 1) * qp, lanes // qp, width), bf),
         "xo": pltpu.VMEM((max(nx - 1, 1) * owned, rows, width), bf),
         "xi": pltpu.VMEM((max(nx - 1, 1) * owned, rows, width), bf),
         "co": pltpu.VMEM((owned, rows, width), bf),
@@ -61,8 +60,8 @@
         "sent": dma((13,)),
         "got": dma((8,)),
         "near": dma((7,)),
-        "yr": dma((max(ny - 1, 1) * qb,)),
-        "zr": dma((max(nz - 1, 1) * qb,)),
+        "yr": dma((max(ny - 1, 1) * qp,)),
+        "zr": dma((max(nz - 1, 1) * qp,)),
         "xr": dma((max(nx - 1, 1) * owned,)),
         "xr2": dma((max(nx - 1, 1) * owned,)),
     }
@@ -77,7 +76,7 @@
     qb, rows, width = q_ref.shape
     owned = p_ref.shape[0]
     ncand = cand_ref.shape[0]
-    lanes = qb * rows
+    lanes, qp, piece = qb * rows, qb * CUTS, rows // CUTS
     scale = 3.0 / math.sqrt(width)
     dp_size = nx * ny
     g, dp = lax.axis_index("group"), lax.axis_index("dp")
@@ -146,12 +145,12 @@
     def query_copy(line, n, device_at, way, t, part):
         src, dst = slots(n, way, t)
         buf = s["q" + line]
-        block = pl.ds(part * rows, rows)
+        block = pl.ds(part * piece, piece)
         return send(
-            q_ref.at[part] if t == 0 else buf.at[src, block],
+            q_ref.at[part // CUTS, pl.ds(part % CUTS * piece, piece)] if t == 0 else buf.at[src, block],
             buf.at[dst, block],
             "yz".index(line),
-            s[line + "r"].at[entry(n, qb, way, t, part)],
+            s[line + "r"].at[entry(n, qp, way, t, part)],
             device_at(1 if way == 0 else n - 1),
         )
 
@@ -173,7 +172,7 @@
             at_x(1 if way == 0 else nx - 1),
         )
 
-    rings = {"y": (ny, y_copy, qb), "z": (nz, z_copy, qb), "x": (nx, x_copy, owned)}
+    rings = {"y": (ny, y_copy, qp), "z": (nz, z_copy, qp), "x": (nx, x_copy, owned)}
 
     def launch(line, kind, t):
         n, copy, parts = rings[line]
@@ -188,12 +187,17 @@
                 copy(way, t, part).wait_recv()
 
     def relay(kind, t):
-        for line in "yz":
-            land(line, kind, t - 1)
-            launch(line, kind, t)
-
-    for line in "yzx":
-        launch(line, "A", 0)
+        for way, part in stream(kind, qp):
+            for line in "yz":
+                n, copy, _ = rings[line]
+                if t - 1 < steps(n, kind):
+                    copy(way, t - 1, part).wait_recv()
+                if t < steps(n, kind):
+                    start(copy(way, t, part))
+
+    for kind in "AB":
+        for line in "yzx":
+            launch(line, kind, 0)
     core_gather = send(p_ref, s["pc"], 3, s["got"].at[0], partner)
     start(core_gather)
 
@@ -204,9 +208,7 @@
     tile_row = lax.broadcasted_iota(jnp.int32, (8, lanes), 0)
     w_row = jnp.concatenate([s["wv"][b : b + 1, :] for b in range(qb)], axis=1) * scale
     pos_row = jnp.concatenate([s["posv"][b : b + 1, :] for b in range(qb)], axis=1).astype(jnp.float32)
-    own_aux = jnp.where(tile_row == 0, w_row, jnp.where(tile_row == 1, pos_row, 0.0))
-    s["auxy"][0] = own_aux
-    s["auxz"][0] = own_aux
+    s["yst"][ny : ny + 8] = jnp.where(tile_row == 0, w_row, jnp.where(tile_row == 1, pos_row, 0.0))
 
     def spread(n, device_at, src, dst, family):
         for r in range(1, n):
@@ -255,14 +257,10 @@
     for copy in scalars:
         copy.wait()
     lax.fori_loop(0, nz, fill_z, 0)
-    for line in "yz":
-        launch(line, "B", 0)
     for copy in whole_q:
         copy.wait()
     s["qz"][0] = s["qy"][0]
     whole_p.wait()
-    aux_y = spread(ny, at_y, s["auxy"].at[0], s["auxy"], 4)
-    aux_z = spread(nz, at_z, s["auxz"].at[0], s["auxz"], 5)
 
     lane = lax.broadcasted_iota(jnp.int32, (1, lanes), 1)
 
@@ -306,7 +304,6 @@
     relay("A", 1)
     lax.fori_loop(0, ny // 2, fill_y, 0)
     relay("B", 1)
-    launch("x", "B", 0)
     lax.fori_loop(ny // 2, ny, fill_y, 0)
     relay("A", 2)
     for t in range(1, half_x):
@@ -368,10 +365,8 @@
     stat = merge([s["sy"][h] for h in range(nx)])
     ring_row = lax.broadcasted_iota(jnp.int32, (ny, lanes), 0)
     stat = jnp.where(ring_row == 0, merge([stat, jnp.broadcast_to(z_row, stat.shape)]), stat)
-    s["yst"][...] = stat
+    s["yst"][0:ny] = stat
     stat_y = spread(ny, at_y, s["yst"], s["ysr"], 7)
-    aux_y()
-    aux_z()
     stat_y()
 
     def turned(value, places):
@@ -379,10 +374,14 @@
             return pltpu.roll(value, places, axis=0)
         return jnp.concatenate([value[ny - places :], value[: ny - places]], axis=0)
 
-    total = merge([stat] + [turned(s["ysr"][j], j) for j in range(1, ny)])
+    total = merge([stat] + [turned(s["ysr"][j, 0:ny], j) for j in range(1, ny)])
     s["ya"][...] = total
-    s["fin"][...] = jnp.broadcast_to(total[0:1, :], (8, lanes))
+    w_row, pos_row = s["yst"][ny : ny + 1, :], s["yst"][ny + 1 : ny + 2, :]
+    fin = jnp.where(tile_row == 1, w_row, jnp.where(tile_row == 2, pos_row, 0.0))
+    s["fin"][...] = jnp.where(tile_row == 0, total[0:1, :], fin)
     fin_z = spread(nz, at_z, s["fin"], s["zfr"], 8)
+
+    s["ysr"][0] = s["yst"][...]
 
     down = lax.broadcasted_iota(jnp.int32, (rows, lanes), 0).astype(jnp.float32)
 
@@ -398,8 +397,8 @@
             entry_y(h, r),
             s["my"][h, pl.ds(r, 1), :],
             s["ya"][pl.ds(r, 1), :],
-            s["auxy"][r, 0:1, :],
-            s["auxy"][r, 1:2, :],
+            s["ysr"][r, ny : ny + 1, :],
+            s["ysr"][r, ny + 1 : ny + 2, :],
         )
 
     def dscore_z(h, r, a_row):
@@ -408,8 +407,8 @@
             entry_z(h, r),
             s["mz"][h, pl.ds(r, 1), :],
             a_row,
-            s["auxz"][r, 0:1, :],
-            s["auxz"][r, 1:2, :],
+            s["zfr"][r, 1:2, :],
+            s["zfr"][r, 2:3, :],
         )
 
     def term(h, r, index, q):
@@ -425,7 +424,7 @@
         out[r] = lax.dot_general(left, right, (((0,), (0,)), ((), ())), preferred_element_type=jnp.float32)
 
     def reduce_copy(line, n, device_at, way, t, part):
-        place = entry(n, owned if line == "x" else qb, way, t - 1, part)
+        place = entry(n, owned if line == "x" else qp, way, t - 1, part)
         return send(
             s[line + "o"].at[place],
             s[line + "i"].at[place],
@@ -435,21 +434,21 @@
         )
 
     def came(line, n, way, t, part):
-        return s[line + "i"][entry(n, owned if line == "x" else qb, way, t - 1, part)].astype(jnp.float32)
+        return s[line + "i"][entry(n, owned if line == "x" else qp, way, t - 1, part)].astype(jnp.float32)
 
     def reduce_send(line, n, device_at, way, t, part, value, alone):
         if not alone:
             reduce_copy(line, n, device_at, way, t + 1, part).wait_recv()
             value = value + came(line, n, way, t + 1, part)
-        s[line + "o"][entry(n, owned if line == "x" else qb, way, t - 1, part)] = value.astype(jnp.bfloat16)
+        s[line + "o"][entry(n, owned if line == "x" else qp, way, t - 1, part)] = value.astype(jnp.bfloat16)
         start(reduce_copy(line, n, device_at, way, t, part))
 
     def query_send(line, kind, t):
         n, device_at = (ny, at_y) if line == "y" else (nz, at_z)
         if 1 <= t <= steps(n, kind):
-            for way, part in stream(kind, qb):
+            for way, part in stream(kind, qp):
                 target = t if way == 0 else (n - t) % n
-                value = s["gq" + line][target, pl.ds(part * rows, rows), :]
+                value = s["gq" + line][target, pl.ds(part * piece, piece), :]
                 reduce_send(line, n, device_at, way, t, part, value, t == steps(n, kind))
 
     def passage_send(kind, t):
@@ -553,22 +552,22 @@
     for part in range(owned):
         s["own"][part] = block_sum(0, part) + block_sum(nx, part) + s["ci"][part].astype(jnp.float32)
     results = []
-    for part in range(qb):
-        block = pl.ds(part * rows, rows)
+    for part in range(qp):
+        block = pl.ds(part * piece, piece)
         value = s["gqy"][0, block, :] + s["gqz"][0, block, :]
-        value += arrived("y", ny, at_y, qb, part)
-        value += arrived("z", nz, at_z, qb, part)
-        s["gqo"][part] = value.astype(gq_ref.dtype)
+        value += arrived("y", ny, at_y, qp, part)
+        value += arrived("z", nz, at_z, qp, part)
+        s["gqo"][part // CUTS, pl.ds(part % CUTS * piece, piece)] = value.astype(gq_ref.dtype)
     results.append(fetch(s["gqo"], gq_ref, 0))
     for part in range(owned):
         value = s["own"][part] + arrived("x", nx, at_x, owned, part)
         s["gpo"][part] = value.astype(gp_ref.dtype)
         results.append(fetch(s["gpo"].at[part], gp_ref.at[part], 1 + part))
     if ny > 1:
-        for family, extent in ((0, s["yo"]), (9, s["yo"]), (4, s["auxy"].at[pl.ds(1, ny - 1)]), (7, s["ysr"].at[pl.ds(1, ny - 1)])):
+        for family, extent in ((0, s["yo"]), (9, s["yo"]), (7, s["ysr"].at[pl.ds(1, ny - 1)])):
             all_sent(family, extent)
     if nz > 1:
-        for family, extent in ((1, s["zo"]), (10, s["zo"]), (5, s["auxz"].at[pl.ds(1, nz - 1)])):
+        for family, extent in ((1, s["zo"]), (10, s["zo"])):
             all_sent(family, extent)
         for family, extent in ((6, s["zsr"].at[pl.ds(1, nz - 1)]), (8, s["zfr"].at[pl.ds(1, nz - 1)])):
             all_sent(family, extent)

time: 84.2 us -> 82.7 us (0.982)
  Pallas kernels: 83.3 us -> 81.8 us
    pallas_call x1, Pallas kernels: 81.3 us -> 79.7 us  [shards(): pl.pallas_call(functools.partial(kernel, (nx, ny, nz), tuple(plan)), out_...]
where the time goes in v4:
time: 82.7 us; the launch traced here: 82.4 us
  Pallas kernels  81.8 us (99%)
    pallas_call x1, Pallas kernels, shards(): pl.pallas_call(functools.partial(kernel, (nx, ny, nz), tuple(plan)), out_...  79.7 us
    pallas_call x1, Pallas kernels, shards(): pl.pallas_call(hand_over, out_shape=shapes, in_specs=[left] * 2, out_spec...  2.03 us

profile of v4, /device:TPU:6, one launch (start us, length us, event | category | flops | bytes accessed | tf_op | source)
XLA Modules:
  0.0 82.4 jit_solution(287375621918334753)
XLA Ops:
  0.6 79.7 %shard_map.77 = (bf16[2,128,512]{2,1,0:T(8,128)(2,1)}, bf16[6,128,512]{2,1,0:T(8,128)(2,1)}) custom-call(bf16[2,128,512]{2,1,0:T(8,128)(2,1)} %q_ref.1, bf16[6,128,512]{2,1,0:T(8,128)(2,1)} %p_ref.1, s32[16,1024]{1,0:T(8,128)} %bitcast.1, s32[3072]{0:T(1024)} %own_ref.1, s32[2,128]{1,0:T(2,128)} %pos_ref.1, f32[2,128]{1,0:T(2,128)} %w_ref.1), custom_call_target="tpu_custom_call" | custom-call | tf_op jit(solution)/shard_map/pallas_call | solution.py:612
  80.4 2.0 %shard_map.78 = (bf16[2,128,512]{2,1,0:T(8,128)(2,1)}, bf16[6,128,512]{2,1,0:T(8,128)(2,1)}) custom-call(bf16[2,128,512]{2,1,0:T(8,128)(2,1)} %get-tuple-element.4.gq_in, bf16[6,128,512]{2,1,0:T(8,128)(2,1)} %get-tuple-element.5.gp_in), custom_call_target="tpu_custom_call" | custom-call | tf_op jit(solution)/shard_map/pallas_call | solution.py:622

commit v5 on v4

--- a/solution.py
+++ b/solution.py
@@ -196,7 +196,7 @@
                     start(copy(way, t, part))
 
     for kind in "AB":
-        for line in "yzx":
+        for line in "xyz":
             launch(line, kind, 0)
     core_gather = send(p_ref, s["pc"], 3, s["got"].at[0], partner)
     start(core_gather)
@@ -305,10 +305,10 @@
     lax.fori_loop(0, ny // 2, fill_y, 0)
     relay("B", 1)
     lax.fori_loop(ny // 2, ny, fill_y, 0)
-    relay("A", 2)
     for t in range(1, half_x):
         land("x", "A", t - 1)
         launch("x", "A", t)
+    relay("A", 2)
 
     span = max(ny, nz) + owned
     for h in range(nx + CORES):

time: 82.7 us -> 83.7 us (1.012); the launches traced: 82.4 us -> 82.4 us
  no operation moved by 1% of the time
where the time goes in v5:
time: 83.7 us; the launch traced here: 82.4 us
  Pallas kernels  81.8 us (98%)
    pallas_call x1, Pallas kernels, shards(): pl.pallas_call(functools.partial(kernel, (nx, ny, nz), tuple(plan)), out_...  79.7 us
    pallas_call x1, Pallas kernels, shards(): pl.pallas_call(hand_over, out_shape=shapes, in_specs=[left] * 2, out_spec...  2.03 us

profile of v5, /device:TPU:6, one launch (start us, length us, event | category | flops | bytes accessed | tf_op | source)
XLA Modules:
  0.0 82.4 jit_solution(130461961442261341)
XLA Ops:
  0.6 79.7 %shard_map.77 = (bf16[2,128,512]{2,1,0:T(8,128)(2,1)}, bf16[6,128,512]{2,1,0:T(8,128)(2,1)}) custom-call(bf16[2,128,512]{2,1,0:T(8,128)(2,1)} %q_ref.1, bf16[6,128,512]{2,1,0:T(8,128)(2,1)} %p_ref.1, s32[16,1024]{1,0:T(8,128)} %bitcast.1, s32[3072]{0:T(1024)} %own_ref.1, s32[2,128]{1,0:T(2,128)} %pos_ref.1, f32[2,128]{1,0:T(2,128)} %w_ref.1), custom_call_target="tpu_custom_call" | custom-call | tf_op jit(solution)/shard_map/pallas_call | solution.py:612
  80.4 2.0 %shard_map.78 = (bf16[2,128,512]{2,1,0:T(8,128)(2,1)}, bf16[6,128,512]{2,1,0:T(8,128)(2,1)}) custom-call(bf16[2,128,512]{2,1,0:T(8,128)(2,1)} %get-tuple-element.4.gq_in, bf16[6,128,512]{2,1,0:T(8,128)(2,1)} %get-tuple-element.5.gp_in), custom_call_target="tpu_custom_call" | custom-call | tf_op jit(solution)/shard_map/pallas_call | solution.py:622
